TPU v7x, 256 devices: a whole 4x4x8 slice. The times are simulated.
256 devices in a mesh: dp: 16 (over y, x), context: 16 (over z, core).
Axes of the slice: x: 4, y: 4, z: 8, core: 2. Of those that a mesh axis runs over, the one named last changes fastest.
Arguments:
- query_rows: bfloat16 [16, 3072, 1024], P('dp', 'context'), may hold values from -40 to 40
- key_rows: bfloat16 [16, 3072, 128], P('dp', 'context'), may hold values from -12 to 12
- value_rows: bfloat16 [16, 3072, 128], P('dp', 'context'), may hold values from -6 to 6
- out_grads: bfloat16 [16, 3072, 1024], P('dp', 'context'), may hold values from -16 to 16
- layer_input: bfloat16 [16, 3072, 8192], P('dp', 'context'), may hold values from -6 to 6
- doc_ids: int32 [16, 3072], P('dp'), may hold values from 0 to 7, never falling along the last dimension, each value on 1 to 1536 neighbouring positions
- pair_span: int32 [16], replicated, may hold values from 0 to 15, each once
Outputs:
- grad_qkv: bfloat16 [16, 3072, 1280], P('dp', 'context')
- grad_weight: float32 [8192, 1280], P(('dp', 'context'))
- amax_record: float32 [16, 16, 2], P('dp', 'context')
Inputs may be any that keep to these rules, and one draw needn't show every extreme that they name: doc_ids[b] never falls along positions; each document holds 1 to 1536 positions, one exactly 1536. `pair_span`: each of 0 to 15 once.
All inputs are finite; a program needn't handle non-finite values.
Results may differ from a plain program's by a relative error of at most 0.0056.
Values may be sent and summed in bfloat16 or wider, within the bound.
A program may use at most 64 MiB of HBM per device.

v0:
```python
import math

import jax
import jax.numpy as jnp
import numpy as np
from jax import lax
from jax.sharding import PartitionSpec as P

THETA_BASE = 500000.0
NEG_LARGE = -1e30


def rope_table(seq_len, head_dim):
    inverse_freq = THETA_BASE ** (-2.0 * np.arange(head_dim // 2) / head_dim)
    angles = np.arange(seq_len)[:, None] * inverse_freq[None, :]
    angles = np.concatenate([angles, angles], axis=1)
    return (np.cos(angles).astype(np.float32), np.sin(angles).astype(np.float32))


def stored_positions(pair_span, pairs, span_len):
    block_index = jnp.arange(2 * pairs, dtype=jnp.int32)
    owner_pair = pair_span[block_index // 2]
    span_index = jnp.where(block_index % 2 == 0, owner_pair, 2 * pairs - 1 - owner_pair)
    row_index = jnp.arange(2 * pairs * span_len, dtype=jnp.int32)
    return (span_index[row_index // span_len] * span_len + row_index % span_len, span_index)


def unrotate(grad_rows, cosine, sine_rows):
    half_dim = grad_rows.shape[-1] // 2
    turned = jnp.concatenate([-grad_rows[..., half_dim:], grad_rows[..., :half_dim]], axis=-1)
    return grad_rows * cosine - turned * sine_rows


def fold_rows(columns, weight_term, shard_rows):
    input_part = lax.slice_in_dim(columns, 0, shard_rows.shape[0], axis=0)
    return weight_term + lax.dot_general(
        input_part, shard_rows, (((0,), (0,)), ((), ())), preferred_element_type=jnp.float32
    )


def local(query_rows, key_rows, value_rows, out_grads, layer_input, doc_ids, pair_span):
    shards = lax.axis_size("context")
    replicas = lax.axis_size("dp")
    this_shard = lax.axis_index("context")
    tok_dev = query_rows.shape[1]
    head_dim = key_rows.shape[2]
    head_count = query_rows.shape[2] // head_dim
    model_width = layer_input.shape[2]
    span_len = tok_dev // 2
    seq_len = tok_dev * shards
    key_block = min(512, seq_len)
    block_count = seq_len // key_block
    score_scale = 1.0 / math.sqrt(head_dim)
    qkv_width = (head_count + 2) * head_dim
    positions, span_index = stored_positions(pair_span, shards, span_len)
    own_pos = lax.dynamic_slice_in_dim(positions, this_shard * tok_dev, tok_dev)
    seq_docs = doc_ids[0]
    own_docs = seq_docs[own_pos]
    span_ids = jnp.arange(2 * shards, dtype=jnp.int32)
    holder = (span_index[None, :] == span_ids[:, None]).astype(jnp.int32)
    inverse = jnp.sum(holder * span_ids[None, :], axis=1)
    out_local = jnp.max(jnp.abs(out_grads)).astype(jnp.float32)
    keys_all, values_all = (
        lax.all_gather(key_rows[0], "context", axis=0, tiled=True),
        lax.all_gather(value_rows[0], "context", axis=0, tiled=True),
    )
    keys_seq = keys_all.reshape(2 * shards, span_len, head_dim)[inverse].reshape(seq_len, head_dim)
    values_seq = values_all.reshape(2 * shards, span_len, head_dim)[inverse].reshape(
        seq_len, head_dim
    )
    queries = query_rows[0].reshape(tok_dev * head_count, head_dim)
    out_rows = out_grads[0].reshape(tok_dev * head_count, head_dim)

    def block_mask(block_start):
        key_pos = block_start + jnp.arange(key_block, dtype=jnp.int32)
        key_docs = lax.dynamic_slice_in_dim(seq_docs, block_start, key_block)
        return (key_pos[None, :] <= own_pos[:, None]) & (key_docs[None, :] == own_docs[:, None])

    def block_scores(block_start):
        key_part = lax.dynamic_slice_in_dim(keys_seq, block_start, key_block)
        value_part = lax.dynamic_slice_in_dim(values_seq, block_start, key_block)
        scores = jnp.dot(queries, key_part.T, preferred_element_type=jnp.float32) * score_scale
        dprobs = jnp.dot(out_rows, value_part.T, preferred_element_type=jnp.float32)
        return (
            key_part,
            scores.reshape(tok_dev, head_count, key_block),
            dprobs.reshape(tok_dev, head_count, key_block),
        )

    def stats_step(state_now, block_start):
        allowed = block_mask(block_start)[:, None, :]
        row_top, row_total, weighted = state_now
        key_part, scores, dprobs = block_scores(block_start)
        new_top = jnp.maximum(row_top, jnp.max(jnp.where(allowed, scores, NEG_LARGE), axis=2))
        factor = jnp.exp(row_top - new_top)
        expd = jnp.where(allowed, jnp.exp(scores - new_top[:, :, None]), 0.0)
        state_next = (
            new_top,
            row_total * factor + jnp.sum(expd, axis=2),
            weighted * factor + jnp.sum(expd * dprobs, axis=2),
        )
        return (state_next, None)

    block_starts = jnp.arange(block_count, dtype=jnp.int32) * key_block
    start_state = (
        jnp.full((tok_dev, head_count), NEG_LARGE, jnp.float32),
        jnp.zeros((tok_dev, head_count), jnp.float32),
        jnp.zeros((tok_dev, head_count), jnp.float32),
    )
    (row_top, row_total, weighted), unused = lax.scan(stats_step, start_state, block_starts)
    row_delta = weighted / row_total

    def grad_step(state_now, block_start):
        allowed = block_mask(block_start)[:, None, :]
        grad_q, ds_max = state_now
        key_part, scores, dprobs = block_scores(block_start)
        prob_rows = (
            jnp.where(allowed, jnp.exp(scores - row_top[:, :, None]), 0.0) / row_total[:, :, None]
        )
        dscores = prob_rows * (dprobs - row_delta[:, :, None])
        probs_low = prob_rows.astype(jnp.bfloat16).reshape(tok_dev * head_count, key_block)
        dscores_low = dscores.astype(jnp.bfloat16).reshape(tok_dev * head_count, key_block)
        grad_v = lax.dot_general(
            probs_low, out_rows, (((0,), (0,)), ((), ())), preferred_element_type=jnp.float32
        )
        grad_k = lax.dot_general(
            dscores_low, queries, (((0,), (0,)), ((), ())), preferred_element_type=jnp.float32
        )
        grad_q = grad_q + jnp.dot(dscores_low, key_part, preferred_element_type=jnp.float32)
        return ((grad_q, jnp.maximum(ds_max, jnp.max(jnp.abs(dscores)))), (grad_k, grad_v))

    grad_start = (
        jnp.zeros((tok_dev * head_count, head_dim), jnp.float32),
        jnp.zeros((), jnp.float32),
    )
    (grad_q, ds_max), (key_terms, value_terms) = lax.scan(grad_step, grad_start, block_starts)
    key_terms = key_terms.reshape(2 * shards, span_len, head_dim)[span_index].reshape(
        seq_len, head_dim
    )
    value_terms = value_terms.reshape(2 * shards, span_len, head_dim)[span_index].reshape(
        seq_len, head_dim
    )
    own_k, own_v = (
        lax.psum_scatter(key_terms, "context", scatter_dimension=0, tiled=True),
        lax.psum_scatter(value_terms, "context", scatter_dimension=0, tiled=True),
    )
    cos_tab, sin_tab = rope_table(seq_len, head_dim)
    cosine = jnp.asarray(cos_tab)[own_pos]
    sine_rows = jnp.asarray(sin_tab)[own_pos]
    query_grads = unrotate(
        grad_q.reshape(tok_dev, head_count, head_dim) * score_scale,
        cosine[:, None, :],
        sine_rows[:, None, :],
    )
    key_grads = unrotate(own_k * score_scale, cosine, sine_rows)
    grad_rows = jnp.concatenate(
        [query_grads.reshape(tok_dev, head_count * head_dim), key_grads, own_v], axis=1
    ).astype(jnp.bfloat16)
    out_max, ds_global = lax.pmax((out_local, ds_max), ("dp", "context"))
    amax_record = jnp.stack([out_max, ds_global]).reshape(1, 1, 2)
    slice_rows = model_width // (replicas * shards)
    inputs = layer_input[0].reshape(tok_dev, replicas, shards, slice_rows)
    columns = lax.all_to_all(inputs, "context", split_axis=2, concat_axis=0, tiled=True).reshape(
        shards * tok_dev, replicas * slice_rows
    )
    zero_term = jnp.zeros((replicas * slice_rows, qkv_width), jnp.float32)
    weight_term = fold_rows(
        columns, zero_term, lax.all_gather(grad_rows, "context", axis=0, tiled=True)
    )
    grad_weight = lax.psum_scatter(weight_term, "dp", scatter_dimension=0, tiled=True)
    return (grad_rows.reshape(1, tok_dev, qkv_width), grad_weight, amax_record)


def solution(mesh):
    in_specs = (
        P("dp", "context", None),
        P("dp", "context", None),
        P("dp", "context", None),
        P("dp", "context", None),
        P("dp", "context", None),
        P("dp", None),
        P(),
    )
    out_specs = (P("dp", "context", None), P(("dp", "context"), None), P("dp", "context", None))
    return jax.shard_map(local, mesh=mesh, in_specs=in_specs, out_specs=out_specs, check_vma=False)
```

profile of v0, /device:TPU:32, one launch (start us, length us, event | category | flops | bytes accessed | tf_op | source)
XLA Modules:
  0.0 690.9 jit_solution(9705693384721259209)
XLA Ops:
  13.1 4.3 compare_select_fusion.1
  17.5 13.1 %select_select_fusion = s32[3072]{0:T(1024)S(1)} fusion(pred[3072]{0:T(1024)(128)(4,1)S(1)} %compare_reduce_fusion.4, pred[3072]{0:T(1024)(128)(4,1)S(1)} %compare_reduce_fusion.5, pred[3072]{0:T(1024)(128)(4,1)S(1)} %compare_reduce_fusion.6, pred[3072]{0:T(1024)(128)(4,1)S(1)} %compare_reduce_fusion.7, pred[3072]{0:T(1024)(128)(4,1)S(1)} %compare_reduce_fusion.8, ...), kind=kLoop, calls=%fused_computation.111 | loop fusion | flops 64512 | bytes 89172 | tf_op jit(solution)/shard_map/gather | solution.py:25
  30.6 2.7 compare_select_fusion.7
  36.3 20.2 %all-gather = bf16[1,3072,128]{2,1,0:T(8,128)(2,1)S(1)} all-gather(bf16[1,192,128]{2,1,0:T(8,128)(2,1)} %param.14), channel_id=2, replica_groups=mesh['dp'=16,'context'=16] {'context'}, dimensions={1}, use_global_device_ids=true | all-gather | bytes 835584 | tf_op jit(solution)/shard_map/all_gather | solution.py:64
  56.5 18.7 %all-gather.1 = bf16[1,3072,128]{2,1,0:T(8,128)(2,1)S(1)} all-gather(bf16[1,192,128]{2,1,0:T(8,128)(2,1)S(1)} %copy-done.16), channel_id=3, replica_groups=mesh['dp'=16,'context'=16] {'context'}, dimensions={1}, use_global_device_ids=true | all-gather | bytes 835584 | tf_op jit(solution)/shard_map/all_gather | solution.py:65
  80.3 138.4 %while.33 = (s32[]{:T(128)}, f32[192,8]{1,0:T(8,128)}, f32[192,8]{1,0:T(8,128)}, f32[192,8]{1,0:T(8,128)}, s32[6]{0:T(128)}, /*index=5*/s32[192]{0:T(256)S(1)}, ...) while((s32[]{:T(128)}, f32[192,8]{1,0:T(8,128)}, ...), condition=%wide.region_5.6_spmd.clone, body=%wide.region_1.5_spmd.clone.sunk | while | flops 410823680 | bytes 21890864 | solution.py:110
  94.2 3.0 fusion.87
  117.1 3.0 fusion.87
  140.2 3.0 fusion.87
  163.3 3.0 fusion.87
  186.4 3.0 fusion.87
  209.5 3.0 fusion.87
  221.9 92.5 %while.34 = (s32[]{:T(128)}, f32[1536,128]{1,0:T(8,128)}, f32[]{:T(128)}, f32[6,512,128]{2,1,0:T(8,128)}, f32[6,512,128]{2,1,0:T(8,128)}, /*index=5*/s32[6]{0:T(...) while((s32[]{:T(128)}, f32[1536,128]{1,0:T(8,128)}, ...), condition=%wide.wide.region_8.9_spmd.clone, body=%wide.wide.region_6.8_spmd.clone.sunk | while | flops 1015185920 | bytes 29456260 | solution.py:136
  314.3 3.3 gather_fusion.6
  317.7 3.5 gather_fusion.7
  327.3 45.2 %reduce-scatter.6.cloned.1.call-done = f32[192,128]{1,0:T(8,128)} async-done(((f32[3072,128]{1,0:T(8,128)}), f32[192,128]{1,0:T(8,128)}) %reduce-scatter.6.cloned.1.call-update) | async-done | bytes 98320 | tf_op jit(solution)/shard_map/reduce_scatter | solution.py:144
  377.0 55.6 %reduce-scatter.8.cloned.1.call-done = f32[192,128]{1,0:T(8,128)} async-done(((f32[3072,128]{1,0:T(8,128)}), f32[192,128]{1,0:T(8,128)}) %reduce-scatter.8.cloned.1.call-update) | async-done | bytes 98320 | tf_op jit(solution)/shard_map/reduce_scatter | solution.py:145
  435.4 4.0 copy.29
  442.0 134.8 %all_to_all.15 = bf16[192,16,16,32]{0,3,1,2:T(8,128)(2,1)S(1)} all-to-all(bf16[192,16,16,32]{0,3,1,2:T(8,128)(2,1)S(1)} %copy.30), channel_id=1, replica_groups=mesh['dp'=16,'context'=16] {'context'}, dimensions={2} | all-to-all | bytes 6291456 | tf_op jit(solution)/shard_map/all_to_all | solution.py:163
  576.8 4.9 copy.31
  581.8 6.5 reshape.409
  588.3 8.2 %convolution_bitcast_fusion.2 = f32[512,1280]{0,1:T(8,128)} fusion(bf16[3072,1280]{1,0:T(8,128)(2,1)} %all-gather.4.cloned.1.call-done, bf16[3072,512]{0,1:T(8,128)(2,1)S(1)} %reshape.409), kind=kOutput, calls=%fused_computation.57 | convolution fusion | flops 4026531840 | bytes 13631488 | tf_op jit(solution)/shard_map/dot_general | solution.py:36
  596.6 3.3 copy.33
  600.5 81.1 %all-reduce = (f32[1]{0:T(128)}, f32[1]{0:T(128)}) all-reduce(f32[1]{0:T(128)} %bitcast.56, bf16[1]{0:T(256)(128)(2,1)} %bitcast.70), channel_id=1, replica_groups=mesh['dp'=16,'context'=16] {'dp','context'}, use_global_device_ids=true, to_apply=%region_14.15 | all-reduce | flops 2 | bytes 14 | tf_op jit(solution)/shard_map/pmax | solution.py:159
  (335 shorter events, 221.9 us)
Async XLA Ops:
  7.2 3.0 copy-start
  7.2 49.4 %copy-start.16 = (bf16[1,192,128]{2,1,0:T(8,128)(2,1)S(1)}, bf16[1,192,128]{2,1,0:T(8,128)(2,1)}, u32[]{:S(2)}) copy-start(bf16[1,192,128]{2,1,0:T(8,128)(2,1)} %param.15) | copy-start | bytes 147460
  7.2 365.3 %reduce-scatter.6.cloned.1.call-start = ((), (), s32[]{:S(2)}) async-start(), calls=%async_computation.4 | async-start | bytes 1671168 | tf_op jit(solution)/shard_map/reduce_scatter | solution.py:144
  33.2 45.1 %copy-start.17 = (s32[1024]{0:T(1024)}, s32[1024]{0:T(1024)S(1)}, u32[]{:S(2)}) copy-start(s32[1024]{0:T(1024)S(1)} %pad_clamp_fusion.2) | copy-start | bytes 12292
  33.2 45.1 %copy-start.4 = (s32[1,3072]{1,0:T(1,128)S(1)}, s32[1,3072]{1,0:T(1,128)}, u32[]{:S(2)}) copy-start(s32[1,3072]{1,0:T(1,128)} %param.18) | copy-start | bytes 36868
  94.2 3.0 copy-start.3
  94.2 3.0 copy-start.11
  117.1 3.0 copy-start.3
  117.1 3.0 copy-start.11
  140.2 3.0 copy-start.3
  140.2 3.0 copy-start.11
  186.4 3.0 copy-start.3
  186.4 3.0 copy-start.11
  317.6 3.7 copy-start.18
  317.7 5.7 copy-start.14
  317.7 114.9 %reduce-scatter.8.cloned.1.call-start = ((), (), s32[]{:S(2)}) async-start(), calls=%async_computation.5 | async-start | bytes 1671168 | tf_op jit(solution)/shard_map/reduce_scatter | solution.py:145
  317.7 7.0 %copy-start.8 = (f32[1536,128]{1,0:T(8,128)S(1)}, f32[1536,128]{1,0:T(8,128)}, u32[]{:S(2)}) copy-start(f32[1536,128]{1,0:T(8,128)} %get-tuple-element.155) | copy-start | bytes 2359300
  321.2 267.0 %all-gather.4.cloned.1.call-start = ((), (), s32[]{:S(2)}) async-start(), calls=%async_computation.6 | async-start | bytes 8355840 | tf_op jit(solution)/shard_map/all_gather | solution.py:168
  373.3 62.1 %copy-start.9 = (bf16[1,192,8192]{2,1,0:T(8,128)(2,1)S(1)}, bf16[1,192,8192]{2,1,0:T(8,128)(2,1)}, u32[]{:S(2)}) copy-start(bf16[1,192,8192]{2,1,0:T(8,128)(2,1)} %param.17) | copy-start | bytes 9437188
  435.1 249.2 %reduce-scatter.10.cloned.1.call-start = ((), (), s32[]{:S(2)}) async-start(), calls=%async_computation.7 | async-start | bytes 2785280
  596.5 3.3 copy-start.10
  596.5 87.0 %copy-start.13 = (f32[192,128]{1,0:T(8,128)S(1)}, f32[192,128]{1,0:T(8,128)}, u32[]{:S(2)}) copy-start(f32[192,128]{1,0:T(8,128)} %reduce-scatter.8.cloned.1.call-done) | copy-start | bytes 294916
  596.5 87.0 %copy-start.12 = (bf16[192,128]{1,0:T(8,128)(2,1)S(1)}, bf16[192,128]{1,0:T(8,128)(2,1)}, u32[]{:S(2)}) copy-start(bf16[192,128]{1,0:T(8,128)(2,1)} %get-tuple-element.330) | copy-start | bytes 147460
  596.5 87.8 %copy-start.1 = (s32[16]{0:T(128)S(1)}, s32[16]{0:T(128)}, u32[]{:S(2)}) copy-start(s32[16]{0:T(128)} %param.19) | copy-start | bytes 196
  (29 other events, 56.4 us)
Sparse Core Ops, SparseCore 0:
  317.8 54.6 reduce-scatter.5
  375.0 57.5 reduce-scatter.7
  435.3 142.6 all-gather.3
  600.0 81.2 reduce-scatter.9
where the time goes:
time: 695 us; the launch traced here: 691 us
  blocking collectives  255 us (37%)
  local copies, waits for them, and re-layouts  119 us (17%)
  waiting for transfers between devices  101 us (15%)
  matrix products  92.2 us (13%)
  other arithmetic  81.7 us (12%)
  loops' own time  27.3 us (4%)
  between operations  14.1 us (2%)
    all_to_all x1, blocking collectives, local(): lax.all_to_all(inputs, 'context', split_axis=2, concat_axis=0, tiled=True)  135 us
    pmax x1, blocking collectives, local(): out_max, ds_global = lax.pmax((out_local, ds_max), ('dp', 'context'))  81.1 us
    reduce_scatter x1, waiting for transfers between devices, local(): lax.psum_scatter(value_terms, 'context', scatter_dimension=0, tiled=True)  55.6 us
    reduce_scatter x1, waiting for transfers between devices, local(): lax.psum_scatter(key_terms, 'context', scatter_dimension=0, tiled=True)  45.2 us
    dot_general x12, matrix products, block_scores(): dprobs = jnp.dot(out_rows, value_part.T, preferred_element_type=jnp.float32)  31.9 us
    dot_general x12, matrix products, block_scores(): jnp.dot(queries, key_part.T, preferred_element_type=jnp.float32)  25.6 us
    all_gather x1, blocking collectives, local(): lax.all_gather(key_rows[0], 'context', axis=0, tiled=True)  20.2 us
    gather x27, other arithmetic, stored_positions(): span_index[row_index // span_len] * span_len + row_index % span_len  19.7 us
  transfers between devices with their start and end apart: 4, of which 2 were waited for; matrix products, arithmetic and copies ran while one was open for 5% of the time, Pallas kernels for 0%

commit v1 on v0

v1 whole, which is shorter than its diff:
```python
import math

import jax
import jax.numpy as jnp
import numpy as np
from jax import lax
from jax.experimental import pallas as pl
from jax.experimental.pallas import tpu as pltpu
from jax.sharding import PartitionSpec as P

MESH = pl.DeviceIdType.MESH
THETA_BASE = 500000.0
LOG2E = 1.4426950408889634
NEG_LARGE = -1e30
HEADS, HEAD_DIM, SPAN, KEY_BLOCK = 8, 128, 96, 256
TOKENS = 2 * SPAN
SIDE, DEPTH = 4, 8
PAIRS = 2 * DEPTH
SEQ = PAIRS * TOKENS
Q_WIDTH = HEADS * HEAD_DIM
WIDTH = Q_WIDTH + 2 * HEAD_DIM
LANES = HEADS * SPAN
F32, BF16 = jnp.float32, jnp.bfloat16


class Place:
    def __init__(self):
        dp, context = lax.axis_index("dp"), lax.axis_index("context")
        self.context = context
        self.y, self.x = dp // SIDE, dp % SIDE
        self.z, self.core = context // 2, context % 2
        z_next, z_prev = (self.z + 1) % DEPTH, (self.z + DEPTH - 1) % DEPTH
        self.z_up, self.z_down = (dp, z_next * 2 + self.core), (dp, z_prev * 2 + self.core)
        self.x_up = (self.y * SIDE + (self.x + 1) % SIDE, context)
        self.x_down = (self.y * SIDE + (self.x + SIDE - 1) % SIDE, context)
        self.y_up = ((self.y + 1) % SIDE * SIDE + self.x, context)
        self.y_down = ((self.y + SIDE - 1) % SIDE * SIDE + self.x, context)
        self.sibling = (dp, context + 1 - 2 * self.core)
        self.rings = ((self.x, self.x_up, self.x_down), (self.y, self.y_up, self.y_down))

    def greet(self):
        barrier = pltpu.get_barrier_semaphore()
        peers = (self.z_up, self.z_down, self.x_up, self.x_down, self.y_up, self.y_down, self.sibling)
        for peer in peers:
            pl.semaphore_signal(barrier, inc=1, device_id=peer, device_id_type=MESH)
        pl.semaphore_wait(barrier, len(peers))


class Copies:
    def __init__(self, send, recv):
        self.send, self.recv, self.all = send, recv, []

    def start(self, src, dst, device):
        i = len(self.all)
        copy = pltpu.make_async_remote_copy(
            src_ref=src, dst_ref=dst, send_sem=self.send.at[i], recv_sem=self.recv.at[i],
            device_id=device, device_id_type=MESH,
        )
        copy.start()
        self.all.append(copy)
        return copy

    def finish(self):
        for copy in self.all:
            copy.wait_send()


FRONT_COPIES = 62


def front_kernel(k_ref, v_ref, x_ref, kv_ref, xa_ref, xb_ref, transit, send, recv, local):
    at = Place()
    at.greet()
    copies = Copies(send, recv)
    planes = (k_ref, v_ref)
    own = [pltpu.make_async_copy(planes[p], kv_ref.at[at.context, p], local.at[p]) for p in range(2)]
    up, down, side = {}, {}, []
    for p in range(2):
        dst = kv_ref.at[at.context, p]
        up[1, p] = copies.start(planes[p], dst, at.z_up)
        down[1, p] = copies.start(planes[p], dst, at.z_down)
    for p in range(2):
        side.append(copies.start(planes[p], kv_ref.at[at.context, p], at.sibling))

    def column(yy, xx, part):
        return pl.ds(pl.multiple_of(((yy * SIDE + xx) * 2 + part) * 256, 256), 256)

    columns_of = (lambda dest, j: column(j, dest, 0), lambda dest, j: column(dest, j, 1))
    outs = (xa_ref, xb_ref)
    far, near = {}, []
    for g, (n, right, left) in enumerate(at.rings):
        dest = (n + 2) % SIDE
        for j in range(2):
            far[g, 0, j] = copies.start(x_ref.at[:, columns_of[g](dest, j)], transit.at[g, 0, j], right)
            far[g, 1, j] = copies.start(x_ref.at[:, columns_of[g](dest, j + 2)], transit.at[g, 1, j], left)
    for g, (n, right, left) in enumerate(at.rings):
        for j in range(SIDE):
            dst = outs[g].at[n, :, j * 256:(j + 1) * 256]
            near.append(copies.start(x_ref.at[:, columns_of[g]((n + 1) % SIDE, j)], dst, right))
            near.append(copies.start(x_ref.at[:, columns_of[g]((n + 3) % SIDE, j)], dst, left))
    for g, (n, right, left) in enumerate(at.rings):
        for j in range(SIDE):
            src = x_ref.at[:, columns_of[g](n, j)]
            own.append(pltpu.make_async_copy(src, outs[g].at[n, :, j * 256:(j + 1) * 256], local.at[len(own)]))
    for copy in own:
        copy.start()

    for t in range(1, 5):
        for p in range(2):
            if (t, p) in up:
                up[t, p].wait_recv()
                block = kv_ref.at[(at.z + DEPTH - t) % DEPTH * 2 + at.core, p]
                if t < 3 or (t == 3 and p == 0):
                    up[t + 1, p] = copies.start(block, block, at.z_up)
                side.append(copies.start(block, block, at.sibling))
            if (t, p) in down:
                down[t, p].wait_recv()
                block = kv_ref.at[(at.z + t) % DEPTH * 2 + at.core, p]
                if t < 3 or (t == 3 and p == 1):
                    down[t + 1, p] = copies.start(block, block, at.z_down)
                side.append(copies.start(block, block, at.sibling))
    for g, (n, right, left) in enumerate(at.rings):
        for j in range(2):
            far[g, 0, j].wait_recv()
            dst = outs[g].at[(n + 3) % SIDE, :, j * 256:(j + 1) * 256]
            near.append(copies.start(transit.at[g, 0, j], dst, right))
            far[g, 1, j].wait_recv()
            dst = outs[g].at[(n + 1) % SIDE, :, (j + 2) * 256:(j + 3) * 256]
            near.append(copies.start(transit.at[g, 1, j], dst, left))
    for copy in side + near:
        copy.wait_recv()
    for copy in own:
        copy.wait()
    copies.finish()


def any_spec():
    return pl.BlockSpec(memory_space=pl.ANY)


def vmem_spec():
    return pl.BlockSpec(memory_space=pltpu.VMEM)


def front(keys, values, inputs):
    half = inputs.shape[1] // 8
    return pl.pallas_call(
        front_kernel,
        out_shape=(
            jax.ShapeDtypeStruct((PAIRS, 2, TOKENS, HEAD_DIM), BF16),
            jax.ShapeDtypeStruct((SIDE, TOKENS, half), BF16),
            jax.ShapeDtypeStruct((SIDE, TOKENS, half), BF16),
        ),
        in_specs=[any_spec()] * 3,
        out_specs=(vmem_spec(),) * 3,
        scratch_shapes=[
            pltpu.VMEM((2, 2, 2, TOKENS, 256), BF16),
            pltpu.SemaphoreType.DMA((FRONT_COPIES,)),
            pltpu.SemaphoreType.DMA((FRONT_COPIES,)),
            pltpu.SemaphoreType.DMA((10,)),
        ],
        compiler_params=pltpu.CompilerParams(collective_id=0, has_side_effects=True, vmem_limit_bytes=12 << 20),
        name="front",
    )(keys, values, inputs)


def trig_tables():
    inverse_freq = THETA_BASE ** (-2.0 * np.arange(HEAD_DIM // 2) / HEAD_DIM)
    freq = np.concatenate([inverse_freq, inverse_freq])
    sign = np.concatenate([np.ones(HEAD_DIM // 2), -np.ones(HEAD_DIM // 2)])
    base = (np.arange(2 * PAIRS) * SPAN)[:, None] * freq[None, :]
    step = np.arange(SPAN)[:, None] * freq[None, :]
    return (
        np.stack([np.cos(base), np.sin(base)]).astype(np.float32),
        np.stack([np.cos(step), np.sin(step)]).astype(np.float32),
        sign.astype(np.float32).reshape(1, HEAD_DIM),
    )


def fold8(x, op):
    out = x[0:8]
    for r in range(8, x.shape[0], 8):
        out = op(out, x[r:r + 8])
    return out


def attention_kernel(
    pair_ref, query_ref, out_ref, kv_ref, docs_ref, row_ref, base_ref, step_ref, sign_ref,
    gq_ref, dkv_ref, trig_ref, top_ref,
    k_pos, v_pos, qs, gs, s_scr, d_scr, dk_acc, dv_acc, dq_acc,
):
    me = lax.axis_index("context")
    scale = 1.0 / math.sqrt(HEAD_DIM)

    def stored_spans():
        for p in range(PAIRS):
            low = pair_ref[p]
            for half, s in ((0, low), (1, 2 * PAIRS - 1 - low)):
                yield p, pl.ds(half * SPAN, SPAN), pl.ds(pl.multiple_of(s * SPAN, 32), SPAN)

    for p, rows, at in stored_spans():
        k_pos[at, :] = kv_ref[p, 0, rows, :]
        v_pos[at, :] = kv_ref[p, 1, rows, :]
    dk_acc[...] = jnp.zeros_like(dk_acc)
    dv_acc[...] = jnp.zeros_like(dv_acc)
    docs_all = docs_ref[:, 0:SPAN]
    starts = [
        jnp.sum(jnp.sum(jnp.where(docs_all < d, 1.0, 0.0), axis=1, keepdims=True), axis=0, keepdims=True)
        for d in range(1, 8)
    ]

    ds_top = jnp.zeros((8, LANES), F32)
    own_low = pair_ref[me]
    for half in range(2):
        s = own_low if half == 0 else 2 * PAIRS - 1 - own_low
        first = half * SPAN
        for h in range(HEADS):
            head = slice(h * HEAD_DIM, (h + 1) * HEAD_DIM)
            qs[h * SPAN:(h + 1) * SPAN, :] = query_ref[first:first + SPAN, head]
            gs[h * SPAN:(h + 1) * SPAN, :] = out_ref[first:first + SPAN, head]
        own_docs = docs_ref[pl.ds(s, 1), :]
        start = jnp.zeros((1, LANES), F32)
        for d in range(1, 8):
            start = jnp.where(own_docs == d, starts[d - 1], start)
        start = start.astype(jnp.int32)
        q_pos = row_ref[...] + s * SPAN
        lo = jnp.min(start) // KEY_BLOCK
        hi = (s * SPAN + SPAN - 1) // KEY_BLOCK + 1
        dq_acc[...] = jnp.zeros_like(dq_acc)

        def block_rows(b):
            return pl.ds(pl.multiple_of(b * KEY_BLOCK, KEY_BLOCK), KEY_BLOCK)

        def score(b, top):
            sc = lax.dot_general(
                k_pos[block_rows(b), :], qs[...], (((1,), (1,)), ((), ())), preferred_element_type=F32
            )
            key_pos = b * KEY_BLOCK + lax.broadcasted_iota(jnp.int32, (KEY_BLOCK, LANES), 0)
            sc = jnp.where((key_pos <= q_pos) & (key_pos >= start), sc, NEG_LARGE)
            s_scr[b] = sc
            return jnp.maximum(top, fold8(sc, jnp.maximum))

        top = lax.fori_loop(lo, hi, score, jnp.full((8, LANES), NEG_LARGE, F32))
        top = jnp.max(top, axis=0, keepdims=True)

        def weigh(b, state):
            total, weighted = state
            dp = lax.dot_general(
                v_pos[block_rows(b), :], gs[...], (((1,), (1,)), ((), ())), preferred_element_type=F32
            )
            e = jnp.exp2((s_scr[b] - top) * (scale * LOG2E))
            s_scr[b] = e
            d_scr[b] = dp
            return total + fold8(e, jnp.add), weighted + fold8(e * dp, jnp.add)

        zero = jnp.zeros((8, LANES), F32)
        total, weighted = lax.fori_loop(lo, hi, weigh, (zero, zero))
        inverse = 1.0 / jnp.sum(total, axis=0, keepdims=True)
        delta = jnp.sum(weighted, axis=0, keepdims=True) * inverse

        def grads(b, high):
            at = block_rows(b)
            p = s_scr[b] * inverse
            ds = p * (d_scr[b] - delta)
            p16, ds16 = p.astype(BF16), ds.astype(BF16)
            dv_acc[at, :] += jnp.dot(p16, gs[...], preferred_element_type=F32)
            dk_acc[at, :] += jnp.dot(ds16, qs[...], preferred_element_type=F32)
            dq_acc[...] += lax.dot_general(
                k_pos[at, :], ds16, (((0,), (0,)), ((), ())), preferred_element_type=F32
            )
            return jnp.maximum(high, fold8(jnp.abs(ds), jnp.maximum))

        ds_top = lax.fori_loop(lo, hi, grads, ds_top)
        cos_a, sin_a = base_ref[0, pl.ds(s, 1), :], base_ref[1, pl.ds(s, 1), :]
        cos_b, sin_b = step_ref[0], step_ref[1]
        cosine = cos_a * cos_b - sin_a * sin_b
        sine = (sin_a * cos_b + cos_a * sin_b) * sign_ref[...]
        trig_ref[0, first:first + SPAN, :] = cosine
        trig_ref[1, first:first + SPAN, :] = sine
        dq = dq_acc[...].T * scale
        for h in range(HEADS):
            v = dq[h * SPAN:(h + 1) * SPAN, :]
            turned = v * cosine + pltpu.roll(v, HEAD_DIM // 2, 1) * sine
            gq_ref[first:first + SPAN, h * HEAD_DIM:(h + 1) * HEAD_DIM] = turned.astype(BF16)

    for p, rows, at in stored_spans():
        dkv_ref[p, 0, rows, :] = dk_acc[at, :].astype(dkv_ref.dtype)
        dkv_ref[p, 1, rows, :] = dv_acc[at, :].astype(dkv_ref.dtype)
    out_top = jnp.max(fold8(jnp.abs(out_ref[...].astype(F32)), jnp.maximum))
    lane = lax.broadcasted_iota(jnp.int32, top_ref.shape, 1)
    top_ref[...] = jnp.where(lane == 0, out_top, jnp.max(ds_top))


def attention(pair_span, query, out, kv, docs):
    docs_wide = jnp.tile(docs.reshape(2 * PAIRS, SPAN), (1, HEADS))
    row = jnp.asarray(np.tile(np.arange(SPAN, dtype=np.int32), HEADS).reshape(1, LANES))
    base, step, sign = (jnp.asarray(t) for t in trig_tables())
    return pl.pallas_call(
        attention_kernel,
        out_shape=(
            jax.ShapeDtypeStruct((TOKENS, Q_WIDTH), BF16),
            jax.ShapeDtypeStruct((PAIRS, 2, TOKENS, HEAD_DIM), BF16),
            jax.ShapeDtypeStruct((2, TOKENS, HEAD_DIM), F32),
            jax.ShapeDtypeStruct((8, 128), F32),
        ),
        in_specs=[pl.BlockSpec(memory_space=pltpu.SMEM)] + [vmem_spec()] * 8,
        out_specs=(vmem_spec(),) * 4,
        scratch_shapes=[
            pltpu.VMEM((SEQ, HEAD_DIM), BF16),
            pltpu.VMEM((SEQ, HEAD_DIM), BF16),
            pltpu.VMEM((LANES, HEAD_DIM), BF16),
            pltpu.VMEM((LANES, HEAD_DIM), BF16),
            pltpu.VMEM((SEQ // KEY_BLOCK, KEY_BLOCK, LANES), F32),
            pltpu.VMEM((SEQ // KEY_BLOCK, KEY_BLOCK, LANES), F32),
            pltpu.VMEM((SEQ, HEAD_DIM), F32),
            pltpu.VMEM((SEQ, HEAD_DIM), F32),
            pltpu.VMEM((HEAD_DIM, LANES), F32),
        ],
        compiler_params=pltpu.CompilerParams(vmem_limit_bytes=40 << 20),
        name="attention",
    )(pair_span, query, out, kv, docs_wide, row, base, step, sign)


MIDDLE_COPIES = 64


def middle_kernel(
    gq_ref, dkv_ref, trig_ref, top_ref, gx_ref, gy_ref, rows_ref, high_ref,
    sib, up_send, up_recv, down_send, down_recv, gkv, tops, top_send, send, recv, local,
):
    at = Place()
    at.greet()
    copies = Copies(send, recv)
    gathered = (gx_ref, gy_ref)
    q_cols, kv_cols = pl.ds(0, Q_WIDTH), pl.ds(Q_WIDTH, 2 * HEAD_DIM)
    halves = (pl.ds(0, Q_WIDTH // 2), pl.ds(Q_WIDTH // 2, Q_WIDTH // 2))
    kv_halves = (pl.ds(Q_WIDTH, HEAD_DIM), pl.ds(Q_WIDTH + HEAD_DIM, HEAD_DIM))

    side_top = copies.start(top_ref, tops.at[0], at.sibling)
    sides = {}
    for shift in (4, 5, 3, 6, 2, 7, 1, 0):
        dest = (at.z + shift) % DEPTH
        sides[shift] = copies.start(dkv_ref.at[dest, 1 - at.core], sib.at[dest], at.sibling)
    from_left, from_right = {}, {}
    for g, (n, right, left) in enumerate(at.rings):
        dst = gathered[g].at[n, :, q_cols]
        from_left[g] = copies.start(gq_ref, dst, right)
        from_right[g] = copies.start(gq_ref, dst, left)
    own = [
        pltpu.make_async_copy(gq_ref, gathered[g].at[n, :, q_cols], local.at[g])
        for g, (n, right, left) in enumerate(at.rings)
    ]
    own.append(pltpu.make_async_copy(gq_ref, rows_ref.at[:, q_cols], local.at[2]))
    for copy in own:
        copy.start()

    def part(dest, p):
        return dkv_ref[dest, at.core, p].astype(F32) + sib[dest, p].astype(F32)

    side_top.wait_recv()
    high = jnp.maximum(top_ref[...], tops[0])
    ups, downs, up_tops, down_tops, waiting = {}, {}, {}, {}, []
    for t in range(1, 5):
        shift_up, shift_down = 5 - t, 3 + t
        for shift in {shift_up, shift_down}:
            sides[shift].wait_recv()
        if t > 1:
            up_tops[t - 1].wait_recv()
            down_tops[t - 1].wait_recv()
            top_send[0, t - 1] = jnp.maximum(high, tops[2 * t - 3])
            top_send[1, t - 1] = jnp.maximum(high, tops[2 * t - 2])
        else:
            top_send[0, 0] = high
            top_send[1, 0] = high
        up_tops[t] = copies.start(top_send.at[0, t - 1], tops.at[2 * t - 1], at.z_up)
        down_tops[t] = copies.start(top_send.at[1, t - 1], tops.at[2 * t], at.z_down)
        for p in range(2):
            for up in (True, False):
                if t == 1 and up != (p == 0):
                    continue
                moves, sent, got = (ups, up_send, up_recv) if up else (downs, down_send, down_recv)
                value = part((at.z + (shift_up if up else shift_down)) % DEPTH, p)
                if (t - 1, p) in moves:
                    moves[t - 1, p].wait_recv()
                    value = value + got[t - 2, p].astype(F32)
                sent[t - 1, p] = value.astype(BF16)
                moves[t, p] = copies.start(sent.at[t - 1, p], got.at[t - 1, p], at.z_up if up else at.z_down)
        if t == 3:
            for g, (n, right, left) in enumerate(at.rings):
                from_left[g].wait_recv()
                block = gathered[g].at[(n + 3) % SIDE, :, halves[0]]
                waiting.append(copies.start(block, block, right))
                from_right[g].wait_recv()
                block = gathered[g].at[(n + 1) % SIDE, :, halves[1]]
                waiting.append(copies.start(block, block, left))
    scale = 1.0 / math.sqrt(HEAD_DIM)
    sides[0].wait_recv()
    sums = []
    for p in range(2):
        ups[4, p].wait_recv()
        downs[4, p].wait_recv()
        sums.append(part(at.z, p) + up_recv[3, p].astype(F32) + down_recv[3, p].astype(F32))
    gk = sums[0] * scale
    gk = gk * trig_ref[0] + pltpu.roll(gk, HEAD_DIM // 2, 1) * trig_ref[1]
    gkv[:, 0:HEAD_DIM] = gk.astype(BF16)
    gkv[:, HEAD_DIM:] = sums[1].astype(BF16)
    from_left, from_right = {}, {}
    for g, (n, right, left) in enumerate(at.rings):
        dst = gathered[g].at[n, :, kv_cols]
        from_left[g] = copies.start(gkv, dst, right)
        from_right[g] = copies.start(gkv, dst, left)
    up_tops[4].wait_recv()
    down_tops[4].wait_recv()
    high = jnp.maximum(jnp.maximum(high, tops[7]), tops[8])
    top_send[0, 4] = high
    x_left = copies.start(top_send.at[0, 4], tops.at[9], at.x_up)
    x_right = copies.start(top_send.at[0, 4], tops.at[10], at.x_down)
    rows_ref[:, kv_cols] = gkv[...]
    for g, (n, right, left) in enumerate(at.rings):
        gathered[g][n, :, kv_cols] = gkv[...]
    for g, (n, right, left) in enumerate(at.rings):
        from_left[g].wait_recv()
        block = gathered[g].at[(n + 3) % SIDE, :, kv_halves[0]]
        waiting.append(copies.start(block, block, right))
        from_right[g].wait_recv()
        block = gathered[g].at[(n + 1) % SIDE, :, kv_halves[1]]
        waiting.append(copies.start(block, block, left))
    x_left.wait_recv()
    x_far = copies.start(tops.at[9], tops.at[11], at.x_up)
    x_right.wait_recv()
    x_far.wait_recv()
    high_ref[...] = jnp.maximum(jnp.maximum(high, tops[9]), jnp.maximum(tops[10], tops[11]))
    for copy in waiting:
        copy.wait_recv()
    for copy in own:
        copy.wait()
    copies.finish()


def middle(gq, dkv, trig, top):
    block = (TOKENS, HEAD_DIM)
    return pl.pallas_call(
        middle_kernel,
        out_shape=(
            jax.ShapeDtypeStruct((SIDE, TOKENS, WIDTH), BF16),
            jax.ShapeDtypeStruct((SIDE, TOKENS, WIDTH), BF16),
            jax.ShapeDtypeStruct((TOKENS, WIDTH), BF16),
            jax.ShapeDtypeStruct((8, 128), F32),
        ),
        in_specs=[vmem_spec()] * 4,
        out_specs=(vmem_spec(),) * 4,
        scratch_shapes=[
            pltpu.VMEM((DEPTH, 2) + block, BF16),
            pltpu.VMEM((4, 2) + block, BF16),
            pltpu.VMEM((4, 2) + block, BF16),
            pltpu.VMEM((4, 2) + block, BF16),
            pltpu.VMEM((4, 2) + block, BF16),
            pltpu.VMEM((TOKENS, 2 * HEAD_DIM), BF16),
            pltpu.VMEM((12, 8, 128), F32),
            pltpu.VMEM((2, 5, 8, 128), F32),
            pltpu.SemaphoreType.DMA((MIDDLE_COPIES,)),
            pltpu.SemaphoreType.DMA((MIDDLE_COPIES,)),
            pltpu.SemaphoreType.DMA((3,)),
        ],
        compiler_params=pltpu.CompilerParams(collective_id=1, has_side_effects=True, vmem_limit_bytes=16 << 20),
        name="middle",
    )(gq, dkv, trig, top)


FINISH_COPIES = 32
SLICE = 32


def finish_kernel(
    pa_ref, pb_ref, top_ref, w_ref, high_ref,
    sib, far_send, far_recv, near_send, near_recv, total, up_send, up_recv, down_send, down_recv, tops,
    send, recv,
):
    at = Place()
    at.greet()
    copies = Copies(send, recv)
    partial = (pa_ref, pb_ref)
    sides = {}
    for hop in (2, 1, 3, 0):
        for g, (n, right, left) in enumerate(at.rings):
            dest = (n + hop) % SIDE
            dest = (at.rings[1 - g][0] + hop) % SIDE
            sides[g, hop] = copies.start(partial[g].at[dest, :, 1 - at.core], sib.at[g, dest], at.sibling)
    y_left = copies.start(top_ref, tops.at[0], at.y_up)
    y_right = copies.start(top_ref, tops.at[1], at.y_down)

    def part(g, dest, rows):
        return partial[g][dest, rows, at.core].astype(F32) + sib[g, dest, rows].astype(F32)

    low, high_half = slice(0, 2), slice(2, 4)
    fars, nears = {}, {}
    for g in range(2):
        n, right, left = at.rings[1 - g]
        dest = (n + 2) % SIDE
        sides[g, 2].wait_recv()
        far_send[g, 0] = part(g, dest, low).astype(BF16)
        fars[g, 0] = copies.start(far_send.at[g, 0], far_recv.at[g, 0], right)
        far_send[g, 1] = part(g, dest, high_half).astype(BF16)
        fars[g, 1] = copies.start(far_send.at[g, 1], far_recv.at[g, 1], left)
    for g in range(2):
        n, right, left = at.rings[1 - g]
        sides[g, 1].wait_recv()
        dest = (n + 1) % SIDE
        near_send[g, 0, 2:4] = part(g, dest, high_half).astype(BF16)
        fars[g, 0].wait_recv()
        near_send[g, 0, 0:2] = (part(g, dest, low) + far_recv[g, 0].astype(F32)).astype(BF16)
        nears[g, 0] = copies.start(near_send.at[g, 0], near_recv.at[g, 0], right)
        sides[g, 3].wait_recv()
        dest = (n + 3) % SIDE
        near_send[g, 1, 0:2] = part(g, dest, low).astype(BF16)
        fars[g, 1].wait_recv()
        near_send[g, 1, 2:4] = (part(g, dest, high_half) + far_recv[g, 1].astype(F32)).astype(BF16)
        nears[g, 1] = copies.start(near_send.at[g, 1], near_recv.at[g, 1], left)
    y_left.wait_recv()
    y_far = copies.start(tops.at[0], tops.at[2], at.y_up)
    for g in range(2):
        n, right, left = at.rings[1 - g]
        sides[g, 0].wait_recv()
        nears[g, 0].wait_recv()
        nears[g, 1].wait_recv()
        total[4 * g:4 * g + 4] = (
            part(g, n, slice(0, 4)) + near_recv[g, 0].astype(F32) + near_recv[g, 1].astype(F32)
        )
    y_right.wait_recv()
    y_far.wait_recv()
    high_ref[...] = jnp.maximum(jnp.maximum(top_ref[...], tops[0]), jnp.maximum(tops[1], tops[2]))

    middle_col = w_ref.shape[1] // 2
    first, second = slice(0, middle_col), slice(middle_col, 2 * middle_col)
    ups, downs = {}, {}
    dest = (at.z + 4) % DEPTH
    up_send[0] = total[dest].astype(BF16)
    ups[1] = copies.start(up_send.at[0, :, pl.ds(0, middle_col)], up_recv.at[0, :, pl.ds(0, middle_col)], at.z_up)
    downs[1] = copies.start(
        up_send.at[0, :, pl.ds(middle_col, middle_col)],
        down_recv.at[0, :, pl.ds(middle_col, middle_col)],
        at.z_down,
    )
    for t in range(2, 5):
        for up in (True, False):
            moves, sent, got, device = (
                (ups, up_send, up_recv, at.z_up) if up else (downs, down_send, down_recv, at.z_down)
            )
            dest = (at.z + (5 - t if up else 3 + t)) % DEPTH
            if t == 2:
                joined, alone = (first, second) if up else (second, first)
                sent[1, :, alone] = total[dest, :, alone].astype(BF16)
                moves[1].wait_recv()
                sent[1, :, joined] = (total[dest, :, joined] + got[0, :, joined].astype(F32)).astype(BF16)
            else:
                moves[t - 1].wait_recv()
                sent[t - 1] = (total[dest] + got[t - 2].astype(F32)).astype(BF16)
            moves[t] = copies.start(sent.at[t - 1], got.at[t - 1], device)
    ups[4].wait_recv()
    downs[4].wait_recv()
    w_ref[...] = total[at.z] + up_recv[3].astype(F32) + down_recv[3].astype(F32)
    copies.finish()


def finish(pa, pb, top):
    quarter = (DEPTH // 2, SLICE, WIDTH)
    return pl.pallas_call(
        finish_kernel,
        out_shape=(jax.ShapeDtypeStruct((SLICE, WIDTH), F32), jax.ShapeDtypeStruct((8, 128), F32)),
        in_specs=[vmem_spec()] * 3,
        out_specs=(vmem_spec(),) * 2,
        scratch_shapes=[
            pltpu.VMEM((2, SIDE) + quarter, BF16),
            pltpu.VMEM((2, 2, 2, SLICE, WIDTH), BF16),
            pltpu.VMEM((2, 2, 2, SLICE, WIDTH), BF16),
            pltpu.VMEM((2, 2) + quarter, BF16),
            pltpu.VMEM((2, 2) + quarter, BF16),
            pltpu.VMEM((DEPTH, SLICE, WIDTH), F32),
            pltpu.VMEM((4, SLICE, WIDTH), BF16),
            pltpu.VMEM((4, SLICE, WIDTH), BF16),
            pltpu.VMEM((4, SLICE, WIDTH), BF16),
            pltpu.VMEM((4, SLICE, WIDTH), BF16),
            pltpu.VMEM((3, 8, 128), F32),
            pltpu.SemaphoreType.DMA((FINISH_COPIES,)),
            pltpu.SemaphoreType.DMA((FINISH_COPIES,)),
        ],
        compiler_params=pltpu.CompilerParams(collective_id=2, has_side_effects=True, vmem_limit_bytes=24 << 20),
        name="finish",
    )(pa, pb, top)


def weight_partial(columns, rows):
    half = columns.shape[2]
    partial = lax.dot_general(
        columns.reshape(SIDE * TOKENS, half),
        rows.reshape(SIDE * TOKENS, WIDTH),
        (((0,), (0,)), ((), ())),
        preferred_element_type=F32,
    )
    return partial.astype(BF16).reshape(SIDE, DEPTH // 2, 2, SLICE, WIDTH)


def local(query_rows, key_rows, value_rows, out_grads, layer_input, doc_ids, pair_span):
    kv, xa, xb = front(key_rows[0], value_rows[0], layer_input[0])
    gq, dkv, trig, top = attention(pair_span, query_rows[0], out_grads[0], kv, doc_ids[0])
    gx, gy, rows, top = middle(gq, dkv.reshape(DEPTH, 2, 2, TOKENS, HEAD_DIM), trig, top)
    weight, top = finish(weight_partial(xa, gx), weight_partial(xb, gy), top)
    return rows[None], weight, top[0:1, 0:2].reshape(1, 1, 2)


def solution(mesh):
    in_specs = (
        P("dp", "context", None),
        P("dp", "context", None),
        P("dp", "context", None),
        P("dp", "context", None),
        P("dp", "context", None),
        P("dp", None),
        P(),
    )
    out_specs = (P("dp", "context", None), P(("dp", "context"), None), P("dp", "context", None))
    return jax.shard_map(local, mesh=mesh, in_specs=in_specs, out_specs=out_specs, check_vma=False)
```

time: 695 us -> 117 us (0.17)
  blocking collectives: 255 us -> 0 us
  local copies, waits for them, and re-layouts: 119 us -> 6.17 us
  Pallas kernels: 0 us -> 105 us
  waiting for transfers between devices: 101 us -> 0 us
  matrix products: 92.2 us -> 4.7 us
  other arithmetic: 81.7 us -> 1.38 us
  loops' own time: 27.3 us -> 0 us
  between operations: 14.1 us -> 0.79 us
    all_to_all x1 -> x0, blocking collectives: 135 us -> none  [local(): lax.all_to_all(inputs, 'context', split_axis=2, concat_axis=0, tiled=True)]
    pallas_call x0 -> x4, Pallas kernels: none -> 105 us  [the longest x1 35.3 us: finish(): pl.pallas_call(finish_kernel, out_shape=(jax.ShapeDtypeStruct((SLICE, WID...]
    reduce_scatter x2 -> x0, waiting for transfers between devices: 101 us -> none  [the longest x1 55.6 us: local(): lax.psum_scatter(value_terms, 'context', scatter_dimension=0, tiled=True)]
    dot_general x43 -> x2, matrix products: 92.2 us -> 4.7 us  [weight_partial(): lax.dot_general(columns.reshape(SIDE * TOKENS, half), rows.reshape(SIDE *...]
    pmax x1 -> x0, blocking collectives: 81.1 us -> none  [local(): out_max, ds_global = lax.pmax((out_local, ds_max), ('dp', 'context'))]
    all_gather x2 -> x0, blocking collectives: 38.9 us -> none  [the longest x1 20.2 us: local(): lax.all_gather(key_rows[0], 'context', axis=0, tiled=True)]
    another operation x2 -> x0, loops' own time: 27.3 us -> none  [the longest x1 15.4 us: local(): lax.scan(grad_step, grad_start, block_starts)]
    gather x31 -> x0, other arithmetic: 20.4 us -> none  [the longest x27 19.7 us: stored_positions(): span_index[row_index // span_len] * span_len + row_index % span_len]
  transfers between devices with their start and end apart: 4 -> 0, of which waited for: 2 -> 0; matrix products, arithmetic and copies ran while one was open for 5% -> 0% of each run, Pallas kernels for 0% -> 0%
where the time goes in v1:
time: 117 us; the launch traced here: 118 us
  Pallas kernels  105 us (90%)
  local copies, waits for them, and re-layouts  6.17 us (5%)
  matrix products  4.7 us (4%)
  other arithmetic  1.38 us (1%)
    pallas_call x1, Pallas kernels, finish(): pl.pallas_call(finish_kernel, out_shape=(jax.ShapeDtypeStruct((SLICE, WID...  35.3 us
    pallas_call x1, Pallas kernels, middle(): pl.pallas_call(middle_kernel, out_shape=(jax.ShapeDtypeStruct((SIDE, TOKE...  28.2 us
    pallas_call x1, Pallas kernels, front(): pl.pallas_call(front_kernel, out_shape=(jax.ShapeDtypeStruct((PAIRS, 2, T...  28 us
    pallas_call x1, Pallas kernels, attention(): pl.pallas_call(attention_kernel, out_shape=(jax.ShapeDtypeStruct((TOKENS,...  13.1 us
    unnamed x23, local copies, waits for them, and re-layouts  5.47 us
    dot_general x2, matrix products, weight_partial(): lax.dot_general(columns.reshape(SIDE * TOKENS, half), rows.reshape(SIDE *...  4.7 us

profile of v1, /device:TPU:32, one launch (start us, length us, event | category | flops | bytes accessed | tf_op | source)
XLA Modules:
  0.0 117.7 jit_solution(6890234907769880689)
XLA Ops:
  0.6 0.0 copy-start.9
  0.6 0.0 copy-start.6
  0.7 0.0 copy-start.7
  0.7 0.0 copy-start.8
  0.7 0.0 copy-start.1
  0.7 0.5 broadcast.5
  1.2 1.4 %reduce.3 = s32[3072]{0:T(1024)S(1)} reduce(s32[1,3072]{1,0:T(1,128)} %param.16, s32[]{:T(128)} %broadcast.5), dimensions={0}, to_apply=%param.16.reduce_sub_computation.3 | reduce | bytes 24580 | tf_op args[5]
  2.6 0.1 tile.10
  2.7 0.1 tile.12.docs_ref
  2.8 0.0 copy-start
  2.8 1.9 %copy-done = bf16[1,192,8192]{2,1,0:T(8,128)(2,1)S(1)} copy-done((bf16[1,192,8192]{2,1,0:T(8,128)(2,1)S(1)}, bf16[1,192,8192]{2,1,0:T(8,128)(2,1)}, u32[]{:S(2)}) %copy-start) | copy-done | bytes 3145752
  4.7 0.8 copy-done.4
  5.5 0.8 copy-done.5
  6.3 28.0 %front.1 = (bf16[16,2,192,128]{3,2,1,0:T(8,128)(2,1)S(1)}, bf16[4,192,1024]{2,1,0:T(8,128)(2,1)S(1)}, bf16[4,192,1024]{2,1,0:T(8,128)(2,1)S(1)}) custom-call(bf16[192,128]{1,0:T(8,128)(2,1)S(1)} %bitcast.26, bf16[192,128]{1,0:T(8,128)(2,1)S(1)} %bitcast.27, bf16[192,8192]{1,0:T(8,128)(2,1)S(1)} %bitcast.19), custom_call_target="tpu_custom_call" | custom-call | tf_op jit(solution)/shard_map/front/pallas_call | solution.py:147
  34.3 0.0 copy-done.9
  34.3 0.0 copy-done.6
  34.4 13.1 %attention.1 = (bf16[192,1024]{1,0:T(8,128)(2,1)S(1)}, bf16[16,2,192,128]{3,2,1,0:T(8,128)(2,1)S(1)}, f32[2,192,128]{2,1,0:T(8,128)S(1)}, f32[8,128]{1,0:T(8,128)S(1)}) custom-call(s32[16]{0:T(128)S(1)} %copy-done.8, bf16[192,1024]{1,0:T(8,128)(2,1)S(1)} %bitcast.24, bf16[192,1024]{1,0:T(8,128)(2,1)S(1)} %bitcast.25, ...), custom_call_target="tpu_custom_call" | custom-call | tf_op jit(solution)/shard_map/attention/pallas_call | solution.py:298
  47.5 28.2 %middle.1 = (bf16[4,192,1280]{2,1,0:T(8,128)(2,1)S(1)}, bf16[4,192,1280]{2,1,0:T(8,128)(2,1)S(1)}, bf16[192,1280]{1,0:T(8,128)(2,1)S(1)}, f32[8,128]{1,0:T(8,128)S(1)}) custom-call(bf16[192,1024]{1,0:T(8,128)(2,1)S(1)} %get-tuple-element.17.gq_ref, bf16[8,2,2,192,128]{4,3,2,1,0:T(8,128)(2,1)S(1)} %bitcast.22, f32[2,192,128]{2,1,0:T(8,128)S(1)} %get-tuple-element.19.trig_ref, ...), custom_call_target="tpu_custom_call" | custom-call | tf_op jit(solution)/shard_map/middle/pallas_call | solution.py:442
  75.7 2.4 %bitcast_convert_fusion.1 = bf16[1024,1280]{1,0:T(8,128)(2,1)S(1)} fusion(bf16[4,192,1024]{2,1,0:T(8,128)(2,1)S(1)} %get-tuple-element.22, bf16[4,192,1280]{2,1,0:T(8,128)(2,1)S(1)} %get-tuple-element.23), kind=kOutput, calls=%fused_computation.1 | convolution fusion | flops 2014576640 | bytes 6160384 | tf_op jit(solution)/shard_map/dot_general | solution.py:594
  78.1 2.3 %bitcast_convert_fusion = bf16[1024,1280]{1,0:T(8,128)(2,1)S(1)} fusion(bf16[4,192,1024]{2,1,0:T(8,128)(2,1)S(1)} %get-tuple-element.24, bf16[4,192,1280]{2,1,0:T(8,128)(2,1)S(1)} %get-tuple-element.25), kind=kOutput, calls=%fused_computation | convolution fusion | flops 2014576640 | bytes 6160384 | tf_op jit(solution)/shard_map/dot_general | solution.py:594
  80.4 35.3 %finish.1 = (f32[32,1280]{1,0:T(8,128)S(1)}, f32[8,128]{1,0:T(8,128)S(1)}) custom-call(bf16[4,4,2,32,1280]{4,3,2,1,0:T(8,128)(2,1)S(1)} %bitcast.20, bf16[4,4,2,32,1280]{4,3,2,1,0:T(8,128)(2,1)S(1)} %bitcast.21, f32[8,128]{1,0:T(8,128)S(1)} %get-tuple-element.26.top_ref), custom_call_target="tpu_custom_call" | custom-call | tf_op jit(solution)/shard_map/finish/pallas_call | solution.py:567
  115.8 0.5 slice_bitcast_fusion
  116.3 0.8 copy.16
  117.1 0.7 copy.17
  (10 shorter events, 0.0 us)
Async XLA Ops:
  0.6 33.7 %copy-start.9 = (f32[1,128]{1,0:T(1,128)S(1)}, f32[1,128]{1,0:T(1,128)}, u32[]{:S(2)}) copy-start(f32[1,128]{1,0:T(1,128)} %constant.11.clone.sign_ref) | copy-start | bytes 1540
  0.6 33.7 %copy-start.6 = (f32[2,32,128]{2,1,0:T(8,128)S(1)}, f32[2,32,128]{2,1,0:T(8,128)}, u32[]{:S(2)}) copy-start(f32[2,32,128]{2,1,0:T(8,128)} %constant.9.clone.base_ref) | copy-start | bytes 98308
  0.7 33.7 %copy-start.7 = (s32[1,768]{1,0:T(1,128)S(1)}, s32[1,768]{1,0:T(1,128)}, u32[]{:S(2)}) copy-start(s32[1,768]{1,0:T(1,128)} %constant.8.clone.row_ref) | copy-start | bytes 9220
  0.7 33.7 %copy-start.8 = (s32[16]{0:T(128)S(1)}, s32[16]{0:T(128)}, u32[]{:S(2)}) copy-start(s32[16]{0:T(128)} %pair_ref.1) | copy-start | bytes 196
  0.7 33.7 %copy-start.1 = (bf16[1,192,1024]{2,1,0:T(8,128)(2,1)S(1)}, bf16[1,192,1024]{2,1,0:T(8,128)(2,1)}, u32[]{:S(2)}) copy-start(bf16[1,192,1024]{2,1,0:T(8,128)(2,1)} %param.11) | copy-start | bytes 1179652
  2.8 1.9 %copy-start = (bf16[1,192,8192]{2,1,0:T(8,128)(2,1)S(1)}, bf16[1,192,8192]{2,1,0:T(8,128)(2,1)}, u32[]{:S(2)}) copy-start(bf16[1,192,8192]{2,1,0:T(8,128)(2,1)} %param.15) | copy-start | bytes 9437188
  4.7 0.8 copy-start.4
  5.5 0.8 copy-start.5
  6.3 28.1 %copy-start.2 = (bf16[1,192,1024]{2,1,0:T(8,128)(2,1)S(1)}, bf16[1,192,1024]{2,1,0:T(8,128)(2,1)}, u32[]{:S(2)}) copy-start(bf16[1,192,1024]{2,1,0:T(8,128)(2,1)} %param.14) | copy-start | bytes 1179652
  6.3 28.1 %copy-start.3 = (f32[2,96,128]{2,1,0:T(8,128)S(1)}, f32[2,96,128]{2,1,0:T(8,128)}, u32[]{:S(2)}) copy-start(f32[2,96,128]{2,1,0:T(8,128)} %constant.10.clone.step_ref) | copy-start | bytes 294916

commit v2 on v1

v2 whole, which is shorter than its diff:
```python
import math

import jax
import jax.numpy as jnp
import numpy as np
from jax import lax
from jax.experimental import pallas as pl
from jax.experimental.pallas import tpu as pltpu
from jax.sharding import PartitionSpec as P

MESH = pl.DeviceIdType.MESH
THETA_BASE = 500000.0
LOG2E = 1.4426950408889634
NEG_LARGE = -1e30
HEADS, HEAD_DIM, SPAN, KEY_BLOCK = 8, 128, 96, 256
TOKENS = 2 * SPAN
SIDE, DEPTH = 4, 8
PAIRS = 2 * DEPTH
SEQ = PAIRS * TOKENS
Q_WIDTH = HEADS * HEAD_DIM
WIDTH = Q_WIDTH + 2 * HEAD_DIM
LANES = HEADS * SPAN
F32, BF16 = jnp.float32, jnp.bfloat16
W_TYPE = BF16


class Place:
    def __init__(self):
        dp, context = lax.axis_index("dp"), lax.axis_index("context")
        self.context = context
        self.y, self.x = dp // SIDE, dp % SIDE
        self.z, self.core = context // 2, context % 2
        z_next, z_prev = (self.z + 1) % DEPTH, (self.z + DEPTH - 1) % DEPTH
        self.z_up, self.z_down = (dp, z_next * 2 + self.core), (dp, z_prev * 2 + self.core)
        self.x_up = (self.y * SIDE + (self.x + 1) % SIDE, context)
        self.x_down = (self.y * SIDE + (self.x + SIDE - 1) % SIDE, context)
        self.y_up = ((self.y + 1) % SIDE * SIDE + self.x, context)
        self.y_down = ((self.y + SIDE - 1) % SIDE * SIDE + self.x, context)
        self.sibling = (dp, context + 1 - 2 * self.core)
        self.rings = ((self.x, self.x_up, self.x_down), (self.y, self.y_up, self.y_down))

    def greet(self):
        barrier = pltpu.get_barrier_semaphore()
        peers = (self.z_up, self.z_down, self.x_up, self.x_down, self.y_up, self.y_down, self.sibling)
        for peer in peers:
            pl.semaphore_signal(barrier, inc=1, device_id=peer, device_id_type=MESH)
        pl.semaphore_wait(barrier, len(peers))


class Copies:
    def __init__(self, send, recv):
        self.send, self.recv, self.all = send, recv, []

    def start(self, src, dst, device):
        i = len(self.all)
        copy = pltpu.make_async_remote_copy(
            src_ref=src, dst_ref=dst, send_sem=self.send.at[i], recv_sem=self.recv.at[i],
            device_id=device, device_id_type=MESH,
        )
        copy.start()
        self.all.append(copy)
        return copy

    def finish(self):
        for copy in self.all:
            copy.wait_send()


FRONT_COPIES = 62


def front_kernel(k_ref, v_ref, x_ref, *refs):
    staged, (kv_ref, xa_ref, xb_ref), held, (transit, send, recv, local) = refs[:4], refs[4:7], refs[7:11], refs[11:]
    at = Place()
    at.greet()
    copies = Copies(send, recv)
    planes = (k_ref, v_ref)
    own = [pltpu.make_async_copy(planes[p], kv_ref.at[at.context, p], local.at[p]) for p in range(2)]
    up, down, side = {}, {}, []
    for p in range(2):
        dst = kv_ref.at[at.context, p]
        up[1, p] = copies.start(planes[p], dst, at.z_up)
        down[1, p] = copies.start(planes[p], dst, at.z_down)
    for p in range(2):
        side.append(copies.start(planes[p], kv_ref.at[at.context, p], at.sibling))

    def column(yy, xx, part):
        return pl.ds(pl.multiple_of(((yy * SIDE + xx) * 2 + part) * 256, 256), 256)

    columns_of = (lambda dest, j: column(j, dest, 0), lambda dest, j: column(dest, j, 1))
    outs = (xa_ref, xb_ref)
    far, near = {}, []
    for g, (n, right, left) in enumerate(at.rings):
        dest = (n + 2) % SIDE
        for j in range(2):
            far[g, 0, j] = copies.start(x_ref.at[:, columns_of[g](dest, j)], transit.at[g, 0, j], right)
            far[g, 1, j] = copies.start(x_ref.at[:, columns_of[g](dest, j + 2)], transit.at[g, 1, j], left)
    for g, (n, right, left) in enumerate(at.rings):
        for j in range(SIDE):
            dst = outs[g].at[n, :, j * 256:(j + 1) * 256]
            near.append(copies.start(x_ref.at[:, columns_of[g]((n + 1) % SIDE, j)], dst, right))
            near.append(copies.start(x_ref.at[:, columns_of[g]((n + 3) % SIDE, j)], dst, left))
    for g, (n, right, left) in enumerate(at.rings):
        for j in range(SIDE):
            src = x_ref.at[:, columns_of[g](n, j)]
            own.append(pltpu.make_async_copy(src, outs[g].at[n, :, j * 256:(j + 1) * 256], local.at[len(own)]))
    def relay_inputs():
        for g, (n, right, left) in enumerate(at.rings):
            for j in range(2):
                far[g, 0, j].wait_recv()
                dst = outs[g].at[(n + 3) % SIDE, :, j * 256:(j + 1) * 256]
                near.append(copies.start(transit.at[g, 0, j], dst, right))
                far[g, 1, j].wait_recv()
                dst = outs[g].at[(n + 1) % SIDE, :, (j + 2) * 256:(j + 3) * 256]
                near.append(copies.start(transit.at[g, 1, j], dst, left))

    for src, dst in zip(staged, held):
        own.append(pltpu.make_async_copy(src, dst, local.at[len(own)]))
    for copy in own:
        copy.start()

    for t in range(1, 5):
        if t == 3:
            relay_inputs()
        for p in range(2):
            if (t, p) in up:
                up[t, p].wait_recv()
                block = kv_ref.at[(at.z + DEPTH - t) % DEPTH * 2 + at.core, p]
                if t < 3 or (t == 3 and p == 0):
                    up[t + 1, p] = copies.start(block, block, at.z_up)
                side.append(copies.start(block, block, at.sibling))
            if (t, p) in down:
                down[t, p].wait_recv()
                block = kv_ref.at[(at.z + t) % DEPTH * 2 + at.core, p]
                if t < 3 or (t == 3 and p == 1):
                    down[t + 1, p] = copies.start(block, block, at.z_down)
                side.append(copies.start(block, block, at.sibling))
    for copy in side + near:
        copy.wait_recv()
    for copy in own:
        copy.wait()
    copies.finish()


def hbm_spec():
    return pl.BlockSpec(memory_space=pltpu.HBM)


def vmem_spec():
    return pl.BlockSpec(memory_space=pltpu.VMEM)


def front(keys, values, inputs, *staged):
    half = inputs.shape[1] // 8
    return pl.pallas_call(
        front_kernel,
        out_shape=(
            jax.ShapeDtypeStruct((PAIRS, 2, TOKENS, HEAD_DIM), BF16),
            jax.ShapeDtypeStruct((SIDE, TOKENS, half), BF16),
            jax.ShapeDtypeStruct((SIDE, TOKENS, half), BF16),
        ) + tuple(jax.ShapeDtypeStruct(a.shape, a.dtype) for a in staged),
        in_specs=[hbm_spec()] * 7,
        out_specs=(vmem_spec(),) * 7,
        scratch_shapes=[
            pltpu.VMEM((2, 2, 2, TOKENS, 256), BF16),
            pltpu.SemaphoreType.DMA((FRONT_COPIES,)),
            pltpu.SemaphoreType.DMA((FRONT_COPIES,)),
            pltpu.SemaphoreType.DMA((14,)),
        ],
        compiler_params=pltpu.CompilerParams(collective_id=0, has_side_effects=True, vmem_limit_bytes=12 << 20),
        name="front",
    )(*(pltpu.with_memory_space_constraint(a, pltpu.HBM) for a in (keys, values, inputs) + staged))


def trig_table():
    inverse_freq = THETA_BASE ** (-2.0 * np.arange(HEAD_DIM // 2) / HEAD_DIM)
    freq = np.concatenate([inverse_freq, inverse_freq])
    sign = np.concatenate([np.ones(HEAD_DIM // 2), -np.ones(HEAD_DIM // 2)])
    base = (np.arange(2 * PAIRS) * SPAN)[:, None] * freq[None, :]
    step = np.arange(SPAN)[:, None] * freq[None, :]
    parts = [np.cos(base), np.sin(base) * sign, np.cos(step), np.sin(step) * sign]
    return np.concatenate(parts).astype(np.float32)


def fold8(x, op):
    out = x[0:8]
    for r in range(8, x.shape[0], 8):
        out = op(out, x[r:r + 8])
    return out


def attention_kernel(
    pair_ref, query_ref, out_ref, kv_ref, docs_ref, table_ref,
    gq_ref, dkv_ref, trig_ref, top_ref,
    k_pos, v_pos, qs, gs, s_scr, d_scr, dk_acc, dv_acc, dq_acc,
):
    me = lax.axis_index("context")
    scale = 1.0 / math.sqrt(HEAD_DIM)

    def stored_spans():
        for p in range(PAIRS):
            low = pair_ref[p]
            for half, s in ((0, low), (1, 2 * PAIRS - 1 - low)):
                yield p, pl.ds(half * SPAN, SPAN), pl.ds(pl.multiple_of(s * SPAN, 32), SPAN)

    for p, rows, at in stored_spans():
        k_pos[at, :] = kv_ref[p, 0, rows, :]
        v_pos[at, :] = kv_ref[p, 1, rows, :]
    dk_acc[...] = jnp.zeros_like(dk_acc)
    dv_acc[...] = jnp.zeros_like(dv_acc)
    docs = docs_ref[...]
    starts = [
        jnp.sum(jnp.where(docs < d, 1.0, 0.0), axis=1, keepdims=True).astype(jnp.int32) for d in range(1, 8)
    ]
    lane = lax.broadcasted_iota(jnp.int32, (1, LANES), 1)
    row = lane - SPAN * ((lane * 683) >> 16)

    ds_top = jnp.zeros((8, LANES), F32)
    own_low = pair_ref[me]
    for half in range(2):
        s = own_low if half == 0 else 2 * PAIRS - 1 - own_low
        first = half * SPAN
        for h in range(HEADS):
            head = slice(h * HEAD_DIM, (h + 1) * HEAD_DIM)
            qs[h * SPAN:(h + 1) * SPAN, :] = query_ref[first:first + SPAN, head]
            gs[h * SPAN:(h + 1) * SPAN, :] = out_ref[first:first + SPAN, head]
        q_pos = row + s * SPAN
        start = jnp.zeros((1, LANES), jnp.int32)
        for first_of in starts:
            start = jnp.where(first_of <= q_pos, jnp.maximum(start, first_of), start)
        lo = jnp.min(start) // KEY_BLOCK
        hi = (s * SPAN + SPAN - 1) // KEY_BLOCK + 1
        dq_acc[...] = jnp.zeros_like(dq_acc)

        def block_rows(b):
            return pl.ds(pl.multiple_of(b * KEY_BLOCK, KEY_BLOCK), KEY_BLOCK)

        def score(b, top):
            sc = lax.dot_general(
                k_pos[block_rows(b), :], qs[...], (((1,), (1,)), ((), ())), preferred_element_type=F32
            )
            key_pos = b * KEY_BLOCK + lax.broadcasted_iota(jnp.int32, (KEY_BLOCK, LANES), 0)
            sc = jnp.where((key_pos <= q_pos) & (key_pos >= start), sc, NEG_LARGE)
            s_scr[b] = sc
            return jnp.maximum(top, fold8(sc, jnp.maximum))

        top = lax.fori_loop(lo, hi, score, jnp.full((8, LANES), NEG_LARGE, F32))
        top = jnp.max(top, axis=0, keepdims=True)

        def weigh(b, state):
            total, weighted = state
            dp = lax.dot_general(
                v_pos[block_rows(b), :], gs[...], (((1,), (1,)), ((), ())), preferred_element_type=F32
            )
            e = jnp.exp2((s_scr[b] - top) * (scale * LOG2E))
            s_scr[b] = e
            d_scr[b] = dp
            return total + fold8(e, jnp.add), weighted + fold8(e * dp, jnp.add)

        zero = jnp.zeros((8, LANES), F32)
        total, weighted = lax.fori_loop(lo, hi, weigh, (zero, zero))
        inverse = 1.0 / jnp.sum(total, axis=0, keepdims=True)
        delta = jnp.sum(weighted, axis=0, keepdims=True) * inverse

        def grads(b, high):
            at = block_rows(b)
            p = s_scr[b] * inverse
            ds = p * (d_scr[b] - delta)
            p16, ds16 = p.astype(BF16), ds.astype(BF16)
            dv_acc[at, :] += jnp.dot(p16, gs[...], preferred_element_type=F32)
            dk_acc[at, :] += jnp.dot(ds16, qs[...], preferred_element_type=F32)
            dq_acc[...] += lax.dot_general(
                k_pos[at, :], ds16, (((0,), (0,)), ((), ())), preferred_element_type=F32
            )
            return jnp.maximum(high, fold8(jnp.abs(ds), jnp.maximum))

        ds_top = lax.fori_loop(lo, hi, grads, ds_top)
        cos_a, sin_a = table_ref[pl.ds(s, 1), :], table_ref[pl.ds(2 * PAIRS + s, 1), :]
        cos_b, sin_b = table_ref[4 * PAIRS:4 * PAIRS + SPAN, :], table_ref[4 * PAIRS + SPAN:, :]
        cosine = cos_a * cos_b - sin_a * sin_b
        sine = sin_a * cos_b + cos_a * sin_b
        trig_ref[0, first:first + SPAN, :] = cosine
        trig_ref[1, first:first + SPAN, :] = sine
        dq = dq_acc[...].T * scale
        for h in range(HEADS):
            v = dq[h * SPAN:(h + 1) * SPAN, :]
            turned = v * cosine + pltpu.roll(v, HEAD_DIM // 2, 1) * sine
            gq_ref[first:first + SPAN, h * HEAD_DIM:(h + 1) * HEAD_DIM] = turned.astype(BF16)

    for p, rows, at in stored_spans():
        dkv_ref[p, 0, rows, :] = dk_acc[at, :].astype(dkv_ref.dtype)
        dkv_ref[p, 1, rows, :] = dv_acc[at, :].astype(dkv_ref.dtype)
    out_top = jnp.max(fold8(jnp.abs(out_ref[...].astype(F32)), jnp.maximum))
    column = lax.broadcasted_iota(jnp.int32, top_ref.shape, 1)
    top_ref[...] = jnp.where(column == 0, out_top, jnp.max(ds_top))


def attention(pair_span, query, out, kv, docs, table):
    return pl.pallas_call(
        attention_kernel,
        out_shape=(
            jax.ShapeDtypeStruct((TOKENS, Q_WIDTH), BF16),
            jax.ShapeDtypeStruct((PAIRS, 2, TOKENS, HEAD_DIM), BF16),
            jax.ShapeDtypeStruct((2, TOKENS, HEAD_DIM), F32),
            jax.ShapeDtypeStruct((8, 128), F32),
        ),
        in_specs=[pl.BlockSpec(memory_space=pltpu.SMEM)] + [vmem_spec()] * 5,
        out_specs=(vmem_spec(),) * 4,
        scratch_shapes=[
            pltpu.VMEM((SEQ, HEAD_DIM), BF16),
            pltpu.VMEM((SEQ, HEAD_DIM), BF16),
            pltpu.VMEM((LANES, HEAD_DIM), BF16),
            pltpu.VMEM((LANES, HEAD_DIM), BF16),
            pltpu.VMEM((SEQ // KEY_BLOCK, KEY_BLOCK, LANES), F32),
            pltpu.VMEM((SEQ // KEY_BLOCK, KEY_BLOCK, LANES), F32),
            pltpu.VMEM((SEQ, HEAD_DIM), F32),
            pltpu.VMEM((SEQ, HEAD_DIM), F32),
            pltpu.VMEM((HEAD_DIM, LANES), F32),
        ],
        compiler_params=pltpu.CompilerParams(vmem_limit_bytes=40 << 20),
        name="attention",
    )(pair_span, query, out, kv, docs, table)


TAIL_COPIES = 140
SLICE = 32
CHUNKS = ((0, 512), (512, 512), (1024, 256))


def tail_kernel(
    gq_ref, dkv_ref, trig_ref, top_ref, xa_ref, xb_ref, rows_ref, w_ref, high_ref,
    gx, gy, turned, sib, up_send, up_recv, down_send, down_recv, gkv, tops, top_send,
    partial, partial_sib, far_send, far_recv, near_send, near_recv, total,
    w_up_send, w_up_recv, w_down_send, w_down_recv, send, recv, local,
):
    at = Place()
    at.greet()
    copies = Copies(send, recv)
    gathered, inputs = (gx, gy), (xa_ref, xb_ref)
    q_cols = pl.ds(0, Q_WIDTH)

    from_left, from_right, spreading = {}, {}, {c: [] for c in range(len(CHUNKS))}

    def spread(c):
        first, width = CHUNKS[c]
        src = gkv if first == Q_WIDTH else gq_ref.at[:, pl.ds(first, width)]
        for g, (n, right, left) in enumerate(at.rings):
            dst = gathered[g].at[n, :, pl.ds(first, width)]
            from_left[g, c] = copies.start(src, dst, right)
            from_right[g, c] = copies.start(src, dst, left)

    def relay(c):
        first, width = CHUNKS[c]
        for g, (n, right, left) in enumerate(at.rings):
            from_left[g, c].wait_recv()
            block = gathered[g].at[(n + 3) % SIDE, :, pl.ds(first, width // 2)]
            spreading[c].append(copies.start(block, block, right))
            from_right[g, c].wait_recv()
            block = gathered[g].at[(n + 1) % SIDE, :, pl.ds(first + width // 2, width // 2)]
            spreading[c].append(copies.start(block, block, left))

    sides = {}

    def part(dest, p):
        return dkv_ref[dest, at.core, p].astype(F32) + sib[dest, p].astype(F32)

    ups, downs, up_tops, down_tops = {}, {}, {}, {}

    def key_value_hop(t, high):
        shift_up, shift_down = 5 - t, 3 + t
        for shift in sorted({shift_up, shift_down}):
            sides[shift].wait_recv()
        for p in range(2):
            for up in (True, False):
                if t == 1 and up != (p == 0):
                    continue
                moves, sent, got = (ups, up_send, up_recv) if up else (downs, down_send, down_recv)
                value = part((at.z + (shift_up if up else shift_down)) % DEPTH, p)
                if (t - 1, p) in moves:
                    moves[t - 1, p].wait_recv()
                    value = value + got[t - 2, p].astype(F32)
                sent[t - 1, p] = value.astype(BF16)
                moves[t, p] = copies.start(sent.at[t - 1, p], got.at[t - 1, p], at.z_up if up else at.z_down)
        if t > 1:
            up_tops[t - 1].wait_recv()
            down_tops[t - 1].wait_recv()
            top_send[0, t - 1] = jnp.maximum(high, tops[2 * t - 3])
            top_send[1, t - 1] = jnp.maximum(high, tops[2 * t - 2])
        else:
            top_send[0, 0] = high
            top_send[1, 0] = high
        up_tops[t] = copies.start(top_send.at[0, t - 1], tops.at[2 * t - 1], at.z_up)
        down_tops[t] = copies.start(top_send.at[1, t - 1], tops.at[2 * t], at.z_down)

    crossing, fars, nears, w_ups, w_downs = {}, {}, {}, {}, {}
    ring = (at.rings[1], at.rings[0])
    low, upper = slice(0, 2), slice(2, 4)

    def turn(g):
        for j in range(SIDE):
            block = inputs[g][:, :, j * 256:(j + 1) * 256].reshape(SIDE * TOKENS, 256)
            turned[g, j] = block.T

    def multiply(c):
        first, width = CHUNKS[c]
        cols = pl.ds(first, width)
        for copy in spreading[c]:
            copy.wait_recv()
        for hop in (2, 1, 3, 0):
            for g in range(2):
                dest = (ring[g][0] + hop) % SIDE
                rows = gathered[g][:, :, cols].reshape(SIDE * TOKENS, width)
                product = jnp.dot(turned[g, dest], rows, preferred_element_type=F32)
                partial[g, dest, :, :, :, cols] = product.astype(BF16).reshape(DEPTH // 2, 2, SLICE, width)
                crossing[g, hop, c] = copies.start(
                    partial.at[g, dest, :, 1 - at.core, :, cols], partial_sib.at[g, dest, :, :, cols], at.sibling
                )

    def w_part(g, dest, rows, cols):
        return partial[g, dest, rows, at.core, :, cols].astype(F32) + partial_sib[g, dest, rows, :, cols].astype(F32)

    def far(c):
        cols = pl.ds(*CHUNKS[c])
        for g in range(2):
            n, right, left = ring[g]
            dest = (n + 2) % SIDE
            crossing[g, 2, c].wait_recv()
            for arm, rows, device in ((0, low, right), (1, upper, left)):
                far_send[g, arm, :, :, cols] = w_part(g, dest, rows, cols).astype(BF16)
                fars[g, arm, c] = copies.start(
                    far_send.at[g, arm, :, :, cols], far_recv.at[g, arm, :, :, cols], device
                )

    def near(c):
        cols = pl.ds(*CHUNKS[c])
        for g in range(2):
            n, right, left = ring[g]
            for arm, hop, device in ((0, 1, right), (1, 3, left)):
                dest = (n + hop) % SIDE
                crossing[g, hop, c].wait_recv()
                joined, alone = (low, upper) if arm == 0 else (upper, low)
                near_send[g, arm, alone, :, cols] = w_part(g, dest, alone, cols).astype(BF16)
                fars[g, arm, c].wait_recv()
                value = w_part(g, dest, joined, cols) + far_recv[g, arm, :, :, cols].astype(F32)
                near_send[g, arm, joined, :, cols] = value.astype(BF16)
                nears[g, arm, c] = copies.start(
                    near_send.at[g, arm, :, :, cols], near_recv.at[g, arm, :, :, cols], device
                )

    def gather_total(c):
        cols = pl.ds(*CHUNKS[c])
        for g in range(2):
            crossing[g, 0, c].wait_recv()
            value = w_part(g, ring[g][0], slice(0, 4), cols)
            for arm in range(2):
                nears[g, arm, c].wait_recv()
                value = value + near_recv[g, arm, :, :, cols].astype(F32)
            total[4 * g:4 * g + 4, :, cols] = value

    def w_hop(t, c):
        first, width = CHUNKS[c]
        cols, half = pl.ds(first, width), width // 2
        sides_of = (pl.ds(first, half), pl.ds(first + half, half))
        for up in (True, False):
            moves, sent, got, device = (
                (w_ups, w_up_send, w_up_recv, at.z_up) if up else (w_downs, w_down_send, w_down_recv, at.z_down)
            )
            dest = (at.z + (5 - t if up else 3 + t)) % DEPTH
            joined, alone = sides_of if up else sides_of[::-1]
            if t == 1:
                sent[0, :, joined] = total[dest, :, joined].astype(W_TYPE)
                moves[1, c] = copies.start(sent.at[0, :, joined], got.at[0, :, joined], device)
                continue
            if t == 2:
                sent[1, :, alone] = total[dest, :, alone].astype(W_TYPE)
                moves[1, c].wait_recv()
                sent[1, :, joined] = (total[dest, :, joined] + got[0, :, joined].astype(F32)).astype(W_TYPE)
            else:
                moves[t - 1, c].wait_recv()
                sent[t - 1, :, cols] = (total[dest, :, cols] + got[t - 2, :, cols].astype(F32)).astype(W_TYPE)
            moves[t, c] = copies.start(sent.at[t - 1, :, cols], got.at[t - 1, :, cols], device)

    def w_end(c):
        cols = pl.ds(*CHUNKS[c])
        w_ups[4, c].wait_recv()
        w_downs[4, c].wait_recv()
        w_ref[:, cols] = total[at.z, :, cols] + w_up_recv[3, :, cols].astype(F32) + w_down_recv[3, :, cols].astype(F32)

    spread(0)
    side_top = copies.start(top_ref, tops.at[0], at.sibling)
    for shift in (4, 5, 3, 6, 2, 7, 1, 0):
        dest = (at.z + shift) % DEPTH
        sides[shift] = copies.start(dkv_ref.at[dest, 1 - at.core], sib.at[dest], at.sibling)
    own = [
        pltpu.make_async_copy(gq_ref, gathered[g].at[n, :, q_cols], local.at[g])
        for g, (n, right, left) in enumerate(at.rings)
    ]
    own.append(pltpu.make_async_copy(gq_ref, rows_ref.at[:, q_cols], local.at[2]))
    for copy in own:
        copy.start()
    side_top.wait_recv()
    high = jnp.maximum(top_ref[...], tops[0])
    key_value_hop(1, high)
    spread(1)
    turn(0)
    key_value_hop(2, high)
    turn(1)
    relay(0)
    key_value_hop(3, high)
    relay(1)
    key_value_hop(4, high)
    for copy in own[0:2]:
        copy.wait()
    multiply(0)

    scale = 1.0 / math.sqrt(HEAD_DIM)
    sides[0].wait_recv()
    sums = []
    for p in range(2):
        ups[4, p].wait_recv()
        downs[4, p].wait_recv()
        sums.append(part(at.z, p) + up_recv[3, p].astype(F32) + down_recv[3, p].astype(F32))
    gk = sums[0] * scale
    gk = gk * trig_ref[0] + pltpu.roll(gk, HEAD_DIM // 2, 1) * trig_ref[1]
    gkv[:, 0:HEAD_DIM] = gk.astype(BF16)
    gkv[:, HEAD_DIM:] = sums[1].astype(BF16)
    spread(2)
    rows_ref[:, Q_WIDTH:] = gkv[...]
    for g, (n, right, left) in enumerate(at.rings):
        gathered[g][n, :, Q_WIDTH:] = gkv[...]
    up_tops[4].wait_recv()
    down_tops[4].wait_recv()
    high = jnp.maximum(jnp.maximum(high, tops[7]), tops[8])
    top_send[0, 4] = high
    x_left = copies.start(top_send.at[0, 4], tops.at[9], at.x_up)
    x_right = copies.start(top_send.at[0, 4], tops.at[10], at.x_down)
    far(0)
    multiply(1)
    relay(2)
    x_left.wait_recv()
    x_far = copies.start(tops.at[9], tops.at[11], at.x_up)
    near(0)
    far(1)
    multiply(2)
    x_right.wait_recv()
    x_far.wait_recv()
    high = jnp.maximum(jnp.maximum(high, tops[9]), jnp.maximum(tops[10], tops[11]))
    top_send[1, 4] = high
    y_left = copies.start(top_send.at[1, 4], tops.at[12], at.y_up)
    y_right = copies.start(top_send.at[1, 4], tops.at[13], at.y_down)
    gather_total(0)
    w_hop(1, 0)
    near(1)
    far(2)
    w_hop(2, 0)
    y_left.wait_recv()
    y_far = copies.start(tops.at[12], tops.at[14], at.y_up)
    gather_total(1)
    w_hop(1, 1)
    near(2)
    w_hop(3, 0)
    w_hop(2, 1)
    w_hop(4, 0)
    gather_total(2)
    w_hop(1, 2)
    w_hop(3, 1)
    w_hop(2, 2)
    w_end(0)
    w_hop(4, 1)
    w_hop(3, 2)
    y_right.wait_recv()
    y_far.wait_recv()
    high_ref[...] = jnp.maximum(jnp.maximum(high, tops[12]), jnp.maximum(tops[13], tops[14]))
    w_end(1)
    w_hop(4, 2)
    own[2].wait()
    w_end(2)
    copies.finish()


def tail(gq, dkv, trig, top, xa, xb):
    block = (TOKENS, HEAD_DIM)
    quarter = (DEPTH // 2, SLICE, WIDTH)
    return pl.pallas_call(
        tail_kernel,
        out_shape=(
            jax.ShapeDtypeStruct((TOKENS, WIDTH), BF16),
            jax.ShapeDtypeStruct((SLICE, WIDTH), F32),
            jax.ShapeDtypeStruct((8, 128), F32),
        ),
        in_specs=[vmem_spec()] * 6,
        out_specs=(vmem_spec(),) * 3,
        scratch_shapes=[
            pltpu.VMEM((SIDE, TOKENS, WIDTH), BF16),
            pltpu.VMEM((SIDE, TOKENS, WIDTH), BF16),
            pltpu.VMEM((2, SIDE, 256, SIDE * TOKENS), BF16),
            pltpu.VMEM((DEPTH, 2) + block, BF16),
            pltpu.VMEM((4, 2) + block, BF16),
            pltpu.VMEM((4, 2) + block, BF16),
            pltpu.VMEM((4, 2) + block, BF16),
            pltpu.VMEM((4, 2) + block, BF16),
            pltpu.VMEM((TOKENS, 2 * HEAD_DIM), BF16),
            pltpu.VMEM((15, 8, 128), F32),
            pltpu.VMEM((2, 5, 8, 128), F32),
            pltpu.VMEM((2, SIDE, DEPTH // 2, 2, SLICE, WIDTH), BF16),
            pltpu.VMEM((2, SIDE) + quarter, BF16),
            pltpu.VMEM((2, 2, 2, SLICE, WIDTH), BF16),
            pltpu.VMEM((2, 2, 2, SLICE, WIDTH), BF16),
            pltpu.VMEM((2, 2) + quarter, BF16),
            pltpu.VMEM((2, 2) + quarter, BF16),
            pltpu.VMEM((DEPTH, SLICE, WIDTH), F32),
            pltpu.VMEM((4, SLICE, WIDTH), W_TYPE),
            pltpu.VMEM((4, SLICE, WIDTH), W_TYPE),
            pltpu.VMEM((4, SLICE, WIDTH), W_TYPE),
            pltpu.VMEM((4, SLICE, WIDTH), W_TYPE),
            pltpu.SemaphoreType.DMA((TAIL_COPIES,)),
            pltpu.SemaphoreType.DMA((TAIL_COPIES,)),
            pltpu.SemaphoreType.DMA((3,)),
        ],
        compiler_params=pltpu.CompilerParams(collective_id=1, has_side_effects=True, vmem_limit_bytes=40 << 20),
        name="tail",
    )(gq, dkv, trig, top, xa, xb)


def local(query_rows, key_rows, value_rows, out_grads, layer_input, doc_ids, pair_span):
    kv, xa, xb, query, out, docs, table = front(
        key_rows[0], value_rows[0], layer_input[0], query_rows[0], out_grads[0], doc_ids, jnp.asarray(trig_table())
    )
    gq, dkv, trig, top = attention(pair_span, query, out, kv, docs, table)
    rows, weight, top = tail(gq, dkv.reshape(DEPTH, 2, 2, TOKENS, HEAD_DIM), trig, top, xa, xb)
    return rows[None], weight, top[0:1, 0:2].reshape(1, 1, 2)


def solution(mesh):
    in_specs = (
        P("dp", "context", None),
        P("dp", "context", None),
        P("dp", "context", None),
        P("dp", "context", None),
        P("dp", "context", None),
        P("dp", None),
        P(),
    )
    out_specs = (P("dp", "context", None), P(("dp", "context"), None), P("dp", "context", None))
    return jax.shard_map(local, mesh=mesh, in_specs=in_specs, out_specs=out_specs, check_vma=False)
```

time: 117 us -> 99.7 us (0.85); the launches traced: 118 us -> 98.3 us
  Pallas kernels: 105 us -> 95.6 us
  matrix products: 4.7 us -> 0 us
  local copies, waits for them, and re-layouts: 6.17 us -> 1.96 us
  other arithmetic: 1.38 us -> 0 us
    pallas_call x1, Pallas kernels: 13.1 us -> 6.31 us  [attention(): pl.pallas_call(attention_kernel, out_shape=(jax.ShapeDtypeStruct((TOKENS,...]
    dot_general x2 -> x0, matrix products: 4.7 us -> none  [weight_partial(): lax.dot_general(columns.reshape(SIDE * TOKENS, half), rows.reshape(SIDE *...]
    unnamed x23 -> x4, local copies, waits for them, and re-layouts: 5.47 us -> 1.45 us
    pallas_call x1, Pallas kernels: 28 us -> 24.8 us  [front(): pl.pallas_call(front_kernel, out_shape=(jax.ShapeDtypeStruct((PAIRS, 2, T...]
    unnamed x1 -> x0, other arithmetic: 1.38 us -> none
    pallas_call x2 -> x1, Pallas kernels: 63.5 us -> 64.5 us  [tail(): pl.pallas_call(tail_kernel, out_shape=(jax.ShapeDtypeStruct((TOKENS, WIDT...]
where the time goes in v2:
time: 99.7 us; the launch traced here: 98.3 us
  Pallas kernels  95.6 us (96%)
  local copies, waits for them, and re-layouts  1.96 us (2%)
    pallas_call x1, Pallas kernels, tail(): pl.pallas_call(tail_kernel, out_shape=(jax.ShapeDtypeStruct((TOKENS, WIDT...  64.5 us
    pallas_call x1, Pallas kernels, front(): pl.pallas_call(front_kernel, out_shape=(jax.ShapeDtypeStruct((PAIRS, 2, T...  24.8 us
    pallas_call x1, Pallas kernels, attention(): pl.pallas_call(attention_kernel, out_shape=(jax.ShapeDtypeStruct((TOKENS,...  6.31 us

profile of v2, /device:TPU:32, one launch (start us, length us, event | category | flops | bytes accessed | tf_op | source)
XLA Modules:
  0.0 98.3 jit_solution(1031378511799045669)
XLA Ops:
  0.6 0.0 copy-start
  0.6 24.8 %front.1 = (bf16[16,2,192,128]{3,2,1,0:T(8,128)(2,1)S(1)}, bf16[4,192,1024]{2,1,0:T(8,128)(2,1)S(1)}, bf16[4,192,1024]{2,1,0:T(8,128)(2,1)S(1)}, bf16[192,1024]{...) custom-call(bf16[192,128]{1,0:T(8,128)(2,1)} %bitcast.14, ...), custom_call_target="tpu_custom_call" | custom-call | tf_op jit(solution)/shard_map/front/pallas_call | solution.py:155
  25.5 0.0 copy-done
  25.5 6.3 %attention.1 = (bf16[192,1024]{1,0:T(8,128)(2,1)S(1)}, bf16[16,2,192,128]{3,2,1,0:T(8,128)(2,1)S(1)}, f32[2,192,128]{2,1,0:T(8,128)S(1)}, f32[8,128]{1,0:T(8,128)S(1)}) custom-call(s32[16]{0:T(128)S(1)} %copy-done, bf16[192,1024]{1,0:T(8,128)(2,1)S(1)} %get-tuple-element.17.query_ref, bf16[192,1024]{1,0:T(8,128)(2,1)S(1)} %get-tuple-element.18.out_ref, ...), custom_call_target="tpu_custom_call" | custom-call | tf_op jit(solution)/shard_map/attention/pallas_call | solution.py:299
  31.8 64.5 %tail.1 = (bf16[192,1280]{1,0:T(8,128)(2,1)S(1)}, f32[32,1280]{1,0:T(8,128)S(1)}, f32[8,128]{1,0:T(8,128)S(1)}) custom-call(bf16[192,1024]{1,0:T(8,128)(2,1)S(1)} %get-tuple-element.22.gq_ref, bf16[8,2,2,192,128]{4,3,2,1,0:T(8,128)(2,1)S(1)} %bitcast.9, f32[2,192,128]{2,1,0:T(8,128)S(1)} %get-tuple-element.24.trig_ref, ...), custom_call_target="tpu_custom_call" | custom-call | tf_op jit(solution)/shard_map/tail/pallas_call | solution.py:584
  96.3 0.5 slice_bitcast_fusion
  96.8 0.8 copy.13
  97.6 0.7 copy.14
Async XLA Ops:
  0.6 24.8 %copy-start = (s32[16]{0:T(128)S(1)}, s32[16]{0:T(128)}, u32[]{:S(2)}) copy-start(s32[16]{0:T(128)} %pair_ref.1) | copy-start | bytes 196

commit v3 on v2

--- a/solution.py
+++ b/solution.py
@@ -39,9 +39,12 @@
         self.sibling = (dp, context + 1 - 2 * self.core)
         self.rings = ((self.x, self.x_up, self.x_down), (self.y, self.y_up, self.y_down))
 
-    def greet(self):
+    def along_z(self, hops):
+        return (lax.axis_index("dp"), (self.z + hops) % DEPTH * 2 + self.core)
+
+    def greet(self, *more):
         barrier = pltpu.get_barrier_semaphore()
-        peers = (self.z_up, self.z_down, self.x_up, self.x_down, self.y_up, self.y_down, self.sibling)
+        peers = (self.z_up, self.z_down, self.x_up, self.x_down, self.y_up, self.y_down, self.sibling) + more
         for peer in peers:
             pl.semaphore_signal(barrier, inc=1, device_id=peer, device_id_type=MESH)
         pl.semaphore_wait(barrier, len(peers))
@@ -192,7 +195,7 @@
 def attention_kernel(
     pair_ref, query_ref, out_ref, kv_ref, docs_ref, table_ref,
     gq_ref, dkv_ref, trig_ref, top_ref,
-    k_pos, v_pos, qs, gs, s_scr, d_scr, dk_acc, dv_acc, dq_acc,
+    k_pos, v_pos, qs, gs, s_scr, d_scr, top_scr, dk_acc, dv_acc, dq_acc,
 ):
     me = lax.axis_index("context")
     scale = 1.0 / math.sqrt(HEAD_DIM)
@@ -235,36 +238,32 @@
         def block_rows(b):
             return pl.ds(pl.multiple_of(b * KEY_BLOCK, KEY_BLOCK), KEY_BLOCK)
 
-        def score(b, top):
+        def weigh(b, state):
+            top, total, weighted = state
             sc = lax.dot_general(
                 k_pos[block_rows(b), :], qs[...], (((1,), (1,)), ((), ())), preferred_element_type=F32
             )
-            key_pos = b * KEY_BLOCK + lax.broadcasted_iota(jnp.int32, (KEY_BLOCK, LANES), 0)
-            sc = jnp.where((key_pos <= q_pos) & (key_pos >= start), sc, NEG_LARGE)
-            s_scr[b] = sc
-            return jnp.maximum(top, fold8(sc, jnp.maximum))
-
-        top = lax.fori_loop(lo, hi, score, jnp.full((8, LANES), NEG_LARGE, F32))
-        top = jnp.max(top, axis=0, keepdims=True)
-
-        def weigh(b, state):
-            total, weighted = state
             dp = lax.dot_general(
                 v_pos[block_rows(b), :], gs[...], (((1,), (1,)), ((), ())), preferred_element_type=F32
             )
-            e = jnp.exp2((s_scr[b] - top) * (scale * LOG2E))
+            d_scr[b] = dp
+            key_pos = b * KEY_BLOCK + lax.broadcasted_iota(jnp.int32, (KEY_BLOCK, LANES), 0)
+            sc = jnp.where((key_pos <= q_pos) & (key_pos >= start), sc, NEG_LARGE)
+            new_top = jnp.maximum(top, jnp.max(fold8(sc, jnp.maximum), axis=0, keepdims=True))
+            e = jnp.exp2((sc - new_top) * (scale * LOG2E))
             s_scr[b] = e
-            d_scr[b] = dp
-            return total + fold8(e, jnp.add), weighted + fold8(e * dp, jnp.add)
+            top_scr[b] = new_top
+            factor = jnp.exp2((top - new_top) * (scale * LOG2E))
+            return new_top, total * factor + fold8(e, jnp.add), weighted * factor + fold8(e * dp, jnp.add)
 
         zero = jnp.zeros((8, LANES), F32)
-        total, weighted = lax.fori_loop(lo, hi, weigh, (zero, zero))
+        top, total, weighted = lax.fori_loop(lo, hi, weigh, (jnp.full((1, LANES), NEG_LARGE, F32), zero, zero))
         inverse = 1.0 / jnp.sum(total, axis=0, keepdims=True)
         delta = jnp.sum(weighted, axis=0, keepdims=True) * inverse
 
         def grads(b, high):
             at = block_rows(b)
-            p = s_scr[b] * inverse
+            p = s_scr[b] * (jnp.exp2((top_scr[b] - top) * (scale * LOG2E)) * inverse)
             ds = p * (d_scr[b] - delta)
             p16, ds16 = p.astype(BF16), ds.astype(BF16)
             dv_acc[at, :] += jnp.dot(p16, gs[...], preferred_element_type=F32)
@@ -313,6 +312,7 @@
             pltpu.VMEM((LANES, HEAD_DIM), BF16),
             pltpu.VMEM((SEQ // KEY_BLOCK, KEY_BLOCK, LANES), F32),
             pltpu.VMEM((SEQ // KEY_BLOCK, KEY_BLOCK, LANES), F32),
+            pltpu.VMEM((SEQ // KEY_BLOCK, 1, LANES), F32),
             pltpu.VMEM((SEQ, HEAD_DIM), F32),
             pltpu.VMEM((SEQ, HEAD_DIM), F32),
             pltpu.VMEM((HEAD_DIM, LANES), F32),
@@ -322,7 +322,7 @@
     )(pair_span, query, out, kv, docs, table)
 
 
-TAIL_COPIES = 140
+TAIL_COPIES = 180
 SLICE = 32
 CHUNKS = ((0, 512), (512, 512), (1024, 256))
 
@@ -331,10 +331,10 @@
     gq_ref, dkv_ref, trig_ref, top_ref, xa_ref, xb_ref, rows_ref, w_ref, high_ref,
     gx, gy, turned, sib, up_send, up_recv, down_send, down_recv, gkv, tops, top_send,
     partial, partial_sib, far_send, far_recv, near_send, near_recv, total,
-    w_up_send, w_up_recv, w_down_send, w_down_recv, send, recv, local,
+    w_up_send, w_up_recv, w_down_send, w_down_recv, last_send, last_recv, send, recv, local,
 ):
     at = Place()
-    at.greet()
+    at.greet(*(at.along_z(k) for k in range(2, DEPTH - 1)))
     copies = Copies(send, recv)
     gathered, inputs = (gx, gy), (xa_ref, xb_ref)
     q_cols = pl.ds(0, Q_WIDTH)
@@ -485,6 +485,24 @@
         w_ups[4, c].wait_recv()
         w_downs[4, c].wait_recv()
         w_ref[:, cols] = total[at.z, :, cols] + w_up_recv[3, :, cols].astype(F32) + w_down_recv[3, :, cols].astype(F32)
+
+    lasts = {}
+
+    def direct(c):
+        first, width = CHUNKS[c]
+        cols, kept = pl.ds(first, width), pl.ds(first - CHUNKS[1][0], width)
+        for k in (4, 3, 5, 2, 6, 1, 7):
+            last_send[k, :, kept] = total[(at.z + k) % DEPTH, :, cols].astype(W_TYPE)
+            lasts[c, k] = copies.start(last_send.at[k, :, kept], last_recv.at[k, :, kept], at.along_z(k))
+
+    def direct_end(c):
+        first, width = CHUNKS[c]
+        cols, kept = pl.ds(first, width), pl.ds(first - CHUNKS[1][0], width)
+        value = total[at.z, :, cols]
+        for k in (1, 7, 2, 6, 3, 5, 4):
+            lasts[c, k].wait_recv()
+            value = value + last_recv[k, :, kept].astype(F32)
+        w_ref[:, cols] = value
 
     spread(0)
     side_top = copies.start(top_ref, tops.at[0], at.sibling)
@@ -536,45 +554,39 @@
     x_right = copies.start(top_send.at[0, 4], tops.at[10], at.x_down)
     far(0)
     multiply(1)
+    far(1)
+    near(0)
     relay(2)
     x_left.wait_recv()
     x_far = copies.start(tops.at[9], tops.at[11], at.x_up)
-    near(0)
-    far(1)
+    near(1)
     multiply(2)
+    far(2)
+    gather_total(0)
+    w_hop(1, 0)
     x_right.wait_recv()
     x_far.wait_recv()
     high = jnp.maximum(jnp.maximum(high, tops[9]), jnp.maximum(tops[10], tops[11]))
     top_send[1, 4] = high
     y_left = copies.start(top_send.at[1, 4], tops.at[12], at.y_up)
     y_right = copies.start(top_send.at[1, 4], tops.at[13], at.y_down)
-    gather_total(0)
-    w_hop(1, 0)
-    near(1)
-    far(2)
+    near(2)
     w_hop(2, 0)
+    gather_total(1)
+    direct(1)
+    w_hop(3, 0)
     y_left.wait_recv()
     y_far = copies.start(tops.at[12], tops.at[14], at.y_up)
-    gather_total(1)
-    w_hop(1, 1)
-    near(2)
-    w_hop(3, 0)
-    w_hop(2, 1)
+    gather_total(2)
+    direct(2)
     w_hop(4, 0)
-    gather_total(2)
-    w_hop(1, 2)
-    w_hop(3, 1)
-    w_hop(2, 2)
-    w_end(0)
-    w_hop(4, 1)
-    w_hop(3, 2)
     y_right.wait_recv()
     y_far.wait_recv()
     high_ref[...] = jnp.maximum(jnp.maximum(high, tops[12]), jnp.maximum(tops[13], tops[14]))
-    w_end(1)
-    w_hop(4, 2)
+    w_end(0)
+    direct_end(1)
+    direct_end(2)
     own[2].wait()
-    w_end(2)
     copies.finish()
 
 
@@ -613,6 +625,8 @@
             pltpu.VMEM((4, SLICE, WIDTH), W_TYPE),
             pltpu.VMEM((4, SLICE, WIDTH), W_TYPE),
             pltpu.VMEM((4, SLICE, WIDTH), W_TYPE),
+            pltpu.VMEM((DEPTH, SLICE, WIDTH - CHUNKS[1][0]), W_TYPE),
+            pltpu.VMEM((DEPTH, SLICE, WIDTH - CHUNKS[1][0]), W_TYPE),
             pltpu.SemaphoreType.DMA((TAIL_COPIES,)),
             pltpu.SemaphoreType.DMA((TAIL_COPIES,)),
             pltpu.SemaphoreType.DMA((3,)),

time: 99.7 us -> 98.8 us (level)
    pallas_call x1, Pallas kernels: 64.5 us -> 60.5 us  [tail(): pl.pallas_call(tail_kernel, out_shape=(jax.ShapeDtypeStruct((TOKENS, WIDT...]
    pallas_call x1, Pallas kernels: 6.31 us -> 9.62 us  [attention(): pl.pallas_call(attention_kernel, out_shape=(jax.ShapeDtypeStruct((TOKENS,...]
where the time goes in v3:
time: 98.8 us; the launch traced here: 97.6 us
  Pallas kernels  95 us (96%)
  local copies, waits for them, and re-layouts  1.96 us (2%)
    pallas_call x1, Pallas kernels, tail(): pl.pallas_call(tail_kernel, out_shape=(jax.ShapeDtypeStruct((TOKENS, WIDT...  60.5 us
    pallas_call x1, Pallas kernels, front(): pl.pallas_call(front_kernel, out_shape=(jax.ShapeDtypeStruct((PAIRS, 2, T...  24.8 us
    pallas_call x1, Pallas kernels, attention(): pl.pallas_call(attention_kernel, out_shape=(jax.ShapeDtypeStruct((TOKENS,...  9.62 us

profile of v3, /device:TPU:32, one launch (start us, length us, event | category | flops | bytes accessed | tf_op | source)
XLA Modules:
  0.0 97.6 jit_solution(4759006872467332327)
XLA Ops:
  0.6 0.0 copy-start
  0.6 24.8 %front.1 = (bf16[16,2,192,128]{3,2,1,0:T(8,128)(2,1)S(1)}, bf16[4,192,1024]{2,1,0:T(8,128)(2,1)S(1)}, bf16[4,192,1024]{2,1,0:T(8,128)(2,1)S(1)}, bf16[192,1024]{...) custom-call(bf16[192,128]{1,0:T(8,128)(2,1)} %bitcast.14, ...), custom_call_target="tpu_custom_call" | custom-call | tf_op jit(solution)/shard_map/front/pallas_call | solution.py:158
  25.5 0.0 copy-done
  25.5 9.6 %attention.1 = (bf16[192,1024]{1,0:T(8,128)(2,1)S(1)}, bf16[16,2,192,128]{3,2,1,0:T(8,128)(2,1)S(1)}, f32[2,192,128]{2,1,0:T(8,128)S(1)}, f32[8,128]{1,0:T(8,128)S(1)}) custom-call(s32[16]{0:T(128)S(1)} %copy-done, bf16[192,1024]{1,0:T(8,128)(2,1)S(1)} %get-tuple-element.17.query_ref, bf16[192,1024]{1,0:T(8,128)(2,1)S(1)} %get-tuple-element.18.out_ref, ...), custom_call_target="tpu_custom_call" | custom-call | tf_op jit(solution)/shard_map/attention/pallas_call | solution.py:298
  35.1 60.5 %tail.1 = (bf16[192,1280]{1,0:T(8,128)(2,1)S(1)}, f32[32,1280]{1,0:T(8,128)S(1)}, f32[8,128]{1,0:T(8,128)S(1)}) custom-call(bf16[192,1024]{1,0:T(8,128)(2,1)S(1)} %get-tuple-element.22.gq_ref, bf16[8,2,2,192,128]{4,3,2,1,0:T(8,128)(2,1)S(1)} %bitcast.9, f32[2,192,128]{2,1,0:T(8,128)S(1)} %get-tuple-element.24.trig_ref, ...), custom_call_target="tpu_custom_call" | custom-call | tf_op jit(solution)/shard_map/tail/pallas_call | solution.py:596
  95.7 0.5 slice_bitcast_fusion
  96.2 0.8 copy.13
  96.9 0.7 copy.14
Async XLA Ops:
  0.6 24.8 %copy-start = (s32[16]{0:T(128)S(1)}, s32[16]{0:T(128)}, u32[]{:S(2)}) copy-start(s32[16]{0:T(128)} %pair_ref.1) | copy-start | bytes 196
